TPU v7x, 32 devices: a whole 2x2x4 slice. The times are simulated.
32 devices in a mesh: groups: 2 (over y), nodes: 16 (over z, x, core).
Axes of the slice: x: 2, y: 2, z: 4, core: 2. Of those that a mesh axis runs over, the one named last changes fastest.
Arguments:
- queries: bfloat16 [4096, 2048], P(('groups', 'nodes')), parts along dimension 0, may hold values from -192 to 192
- seg_kv: bfloat16 [2, 4096, 1024], P(None, ('groups', 'nodes')), parts along dimension 1, may hold values from -6 to 6
- kv_store: bfloat16 [2, 864, 128, 1024], P(None, ('groups', 'nodes')), parts along dimension 1, may hold values from -6 to 6
- seg_parent: int32 [8], P('groups'), parts along dimension 0, may hold values from 0 to 39, as said below
- block_up: int32 [80], P('groups'), parts along dimension 0, may hold values from -1 to 12, as said below
- page_owner: int32 [80, 4], P('groups'), parts along dimension 0, may hold values from 0 to 15, as said below
- page_slot: int32 [80, 4], P('groups'), parts along dimension 0, may hold values from 0 to 26, as said below
Outputs:
- attended: bfloat16 [4096, 2048], P(('groups', 'nodes')), parts along dimension 0
There are 2 independent parts, one for each index of `groups`. A program takes and returns all parts, laid end to end along the dimension named above; each array names one. Nothing has to cross between parts.
Inputs may be any that keep to these rules, and one draw needn't show every extreme that they name: `block_up`: block 0 is the root and alone has -1; every other block's parent has a smaller number and lies one depth above it; depth d holds 3**d blocks, numbered in order of depth. `seg_parent`: some segment's parent is the last block, at depth 4 - 1, so that its path holds 4 blocks. `page_owner`: the pages of the blocks on one segment's path lie on distinct devices, so a device needs at most one page from each device, and some device needs one from every device; a device holds at most 27 pages, and some device holds 27. `page_slot`: no two pages share a device and a slot.
All inputs are finite; a program needn't handle non-finite values.
Results may differ from a plain program's by a relative error of at most 0.0035.
Values may be sent and summed in bfloat16 or wider, within the bound.
No kernel may reach another device: no remote copies, remote signals or barrier semaphores. Data moves between devices by JAX's collectives and lax.ppermute only.
A program may use at most 64 MiB of HBM per device.

v0:
```python
import jax
import jax.numpy as jnp
from jax import lax
from jax.sharding import PartitionSpec as P

HEADS = 16
KV_HEADS = 8
HEAD_DIM = 128
DEPTHS = 4


query_scale = 168.0 ** (-0.5)


def swapped(x, axis, distance):
    return lax.ppermute(x, axis, [(i, i ^ 1 << distance) for i in range(lax.axis_size(axis))])


def walk_paths(seg_parent, block_up):
    chain_list = []
    current = seg_parent
    for depth_step in range(DEPTHS):
        chain_list.append(current)
        safe_blocks = jnp.maximum(current, 0)
        current = jnp.where(current >= 0, block_up[safe_blocks], -1)
    return jnp.stack(chain_list, axis=1)


def join_halves(mine_part, their_part, upper_half, join_axis):
    first_part = jnp.where(upper_half, their_part, mine_part)
    second_part = jnp.where(upper_half, mine_part, their_part)
    return jnp.concatenate([first_part, second_part], axis=join_axis)


def pick_half(array_in, upper_half, pick_axis):
    low_part = lax.index_in_dim(array_in, 0, axis=pick_axis, keepdims=False)
    high_part = lax.index_in_dim(array_in, 1, axis=pick_axis, keepdims=False)
    return (jnp.where(upper_half, high_part, low_part), jnp.where(upper_half, low_part, high_part))


def attend_core(query_block, own_block, anc_block, own_live, anc_live):
    own_scores = (
        jnp.einsum("tkgd,nkd->tkgn", query_block, own_block[0], preferred_element_type=jnp.float32)
        * query_scale
    )
    anc_scores = (
        jnp.einsum("tkgd,nkd->tkgn", query_block, anc_block[0], preferred_element_type=jnp.float32)
        * query_scale
    )
    own_scores = jnp.where(own_live[:, None, None, :], own_scores, -jnp.inf)
    anc_scores = jnp.where(anc_live[None, None, None, :], anc_scores, -jnp.inf)
    row_max = jnp.maximum(jnp.max(own_scores, axis=-1), jnp.max(anc_scores, axis=-1))[..., None]
    own_weights = jnp.exp(own_scores - row_max)
    anc_weights = jnp.exp(anc_scores - row_max)
    weight_sum = jnp.sum(own_weights, axis=-1) + jnp.sum(anc_weights, axis=-1)
    mixed_sum = jnp.einsum(
        "tkgn,nkd->tkgd",
        own_weights.astype(jnp.bfloat16),
        own_block[1],
        preferred_element_type=jnp.float32,
    )
    mixed_sum = mixed_sum + jnp.einsum(
        "tkgn,nkd->tkgd",
        anc_weights.astype(jnp.bfloat16),
        anc_block[1],
        preferred_element_type=jnp.float32,
    )
    return (mixed_sum / weight_sum[..., None]).astype(jnp.bfloat16)


def local(queries, seg_kv, kv_store, seg_parent, block_up, page_owner, page_slot):
    node_count = lax.axis_size("nodes")
    device_index = lax.axis_index("nodes")
    member = device_index % 4
    segment = device_index // 4
    tok_rows = queries.shape[0]
    kv_width = seg_kv.shape[2]
    page_tok = kv_store.shape[2]
    head_group = HEADS // KV_HEADS
    path_blocks = walk_paths(seg_parent, block_up)
    path_live = path_blocks >= 0
    safe_blocks = jnp.maximum(path_blocks, 0)
    owners = page_owner[safe_blocks]
    held_here = (owners == device_index) & path_live[:, :, None]
    slot_pick = jnp.sum(jnp.where(held_here, page_slot[safe_blocks], 0), axis=(1, 2))
    has_page = jnp.any(held_here, axis=(1, 2))
    picked = jnp.take(kv_store, slot_pick, axis=1)
    outgoing = jnp.where(has_page[None, :, None, None], picked, jnp.zeros((), kv_store.dtype))
    my_owners = jnp.take(owners, segment, axis=0)
    my_live = jnp.take(path_live, segment, axis=0)
    matches = my_owners[:, :, None] == jnp.arange(node_count)[None, None, :]
    wanted = jnp.any(matches & my_live[:, None, None], axis=(0, 1))
    anc_live = jnp.repeat(wanted, page_tok)
    kv_quarter = kv_width // 4
    query_quarter = queries.shape[1] // 4
    seg_count = node_count // 4
    sending = outgoing.reshape(2, seg_count, page_tok, 4, kv_quarter)
    sending = jnp.transpose(sending, (0, 1, 3, 2, 4)).reshape(2, node_count, page_tok, kv_quarter)
    arrived = lax.all_to_all(sending, "nodes", split_axis=1, concat_axis=1, tiled=True)
    ancestors = arrived.reshape(2, node_count * page_tok, kv_quarter)
    query_part = queries.reshape(tok_rows, 2, 2, query_quarter)
    kv_part = seg_kv.reshape(2, tok_rows, 2, 2, kv_quarter)
    for bit_index in range(2):
        upper_half = member // 2**bit_index % 2 == 1
        query_keep, query_send = pick_half(query_part, upper_half, query_part.ndim - 2)
        kv_keep, kv_send = pick_half(kv_part, upper_half, kv_part.ndim - 2)
        query_recv, kv_recv = swapped((query_send, kv_send), "nodes", bit_index)
        query_part = join_halves(query_keep, query_recv, upper_half, 0)
        kv_part = join_halves(kv_keep, kv_recv, upper_half, 1)
    segment_rows = 4 * tok_rows
    all_live = jnp.arange(segment_rows)[None, :] <= jnp.arange(segment_rows)[:, None]
    group_cols = head_group * HEAD_DIM

    def attend_head(head_index):
        query_block = lax.dynamic_slice_in_dim(query_part, head_index * group_cols, group_cols, 1)
        query_block = query_block.reshape(segment_rows, 1, head_group, HEAD_DIM)
        own_block = lax.dynamic_slice_in_dim(kv_part, head_index * HEAD_DIM, HEAD_DIM, 2).reshape(
            2, segment_rows, 1, HEAD_DIM
        )
        anc_block = lax.dynamic_slice_in_dim(ancestors, head_index * HEAD_DIM, HEAD_DIM, 2).reshape(
            2, node_count * page_tok, 1, HEAD_DIM
        )
        return attend_core(query_block, own_block, anc_block, all_live, anc_live).reshape(
            segment_rows, group_cols
        )

    per_head = lax.map(attend_head, jnp.arange(kv_quarter // HEAD_DIM))
    result_part = jnp.transpose(per_head, (1, 0, 2)).reshape(4, tok_rows, query_quarter)
    for bit_index in range(2):
        upper_half = member // 2**bit_index % 2 == 1
        shaped = result_part.reshape(-1, 2, tok_rows, result_part.shape[2])
        result_keep, result_send = pick_half(shaped, upper_half, 1)
        result_recv = swapped(result_send, "nodes", bit_index)
        result_part = join_halves(result_keep, result_recv, upper_half, 2)
    return result_part[0]


def solution(mesh):
    in_specs = (
        P(("groups", "nodes"), None),
        P(None, ("groups", "nodes"), None),
        P(None, ("groups", "nodes"), None, None),
        P("groups"),
        P("groups"),
        P("groups", None),
        P("groups", None),
    )
    out_specs = P(("groups", "nodes"), None)
    return jax.shard_map(local, mesh=mesh, in_specs=in_specs, out_specs=out_specs, check_vma=False)
```

profile of v0, /device:TPU:16, one launch (start us, length us, event | category | flops | bytes accessed | tf_op | source)
XLA Modules:
  0.0 116.1 jit_solution(15054207944047625588)
XLA Ops:
  4.5 0.8 copy.217
  6.7 0.8 copy.220
  8.4 5.7 %gather_fusion.5 = bf16[4,2,128,1024]{3,2,1,0:T(8,128)(2,1)S(1)} fusion(bf16[2,27,128,1024]{3,2,1,0:T(8,128)(2,1)} %param.11, s32[1024]{0:T(1024)S(1)} %pad_clamp_fusion), kind=kCustom, calls=%fused_computation.5 | custom fusion | bytes 4194320 | tf_op jit(solution)/shard_map/jit(_take)/gather | solution.py:87
  15.0 1.5 %copy.223 = bf16[2,16,128,256]{3,2,0,1:T(8,128)(2,1)} copy(bf16[2,16,128,256]{3,2,1,0:T(8,128)(2,1)S(1)} %bitcast.257) | data formatting | bytes 4194304 | tf_op jit(solution)/shard_map/reshape | solution.py:98
  16.5 6.3 %all-to-all-start = ((bf16[2,16,128,256]{3,2,0,1:T(8,128)(2,1)}), bf16[2,16,128,256]{3,2,0,1:T(8,128)(2,1)S(1)}, u32[]{:S(2)}, u32[]{:S(2)}) async-start(bf16[2,16,128,256]{3,2,0,1:T(8,128)(2,1)} %copy.223), calls=%async_computation | async-start | bytes 4194304 | tf_op jit(solution)/shard_map/all_to_all | solution.py:99
  23.9 1.3 %copy.199 = bf16[2,128,1024]{1,2,0:T(8,128)(2,1)S(1)} copy(bf16[2,128,1024]{2,1,0:T(8,128)(2,1)} %param.10) | data formatting | bytes 1048576 | tf_op args[1]
  25.2 0.8 fusion.34
  26.8 1.0 broadcast_select_fusion.1
  27.9 1.5 %collective-permute-start.3 = (bf16[256,512]{0,1:T(8,128)(2,1)S(1)}, bf16[256,512]{0,1:T(8,128)(2,1)S(1)}, u32[]{:S(2)}, u32[]{:S(2)}) collective-permute-start(bf16[256,512]{0,1:T(8,128)(2,1)S(1)} %select_bitcast_fusion.2), channel_id=1, source_target_pairs={{0,2},{1,3},{2,0},{3,1},{4,6},{5,7},{6,4},{7,5},{8,10},{9,11},{10,... | collective-permute-start | bytes 786440 | tf_op jit(solution)/shard_map/ppermute | solution.py:16
  30.2 13.5 %collective-permute-done.3 = bf16[256,512]{0,1:T(8,128)(2,1)S(1)} collective-permute-done((bf16[256,512]{0,1:T(8,128)(2,1)S(1)}, bf16[256,512]{0,1:T(8,128)(2,1)S(1)}, u32[]{:S(2)}, u32[]{:S(2)}) %collective-permute-start.3) | collective-permute-done | bytes 262176 | tf_op jit(solution)/shard_map/ppermute | solution.py:16
  43.9 7.3 %collective-permute-done.1 = bf16[2,256,256]{1,2,0:T(8,128)(2,1)S(1)} collective-permute-done((bf16[2,256,256]{1,2,0:T(8,128)(2,1)S(1)}, bf16[2,256,256]{1,2,0:T(8,128)(2,1)S(1)}, u32[]{:S(2)}, u32[]{:S(2)}) %collective-permute-start.1) | collective-permute-done | bytes 262176 | tf_op jit(solution)/shard_map/ppermute | solution.py:16
  51.4 19.0 %all-to-all-done = bf16[2,16,128,256]{3,2,0,1:T(8,128)(2,1)S(1)} async-done(((bf16[2,16,128,256]{3,2,0,1:T(8,128)(2,1)}), bf16[2,16,128,256]{3,2,0,1:T(8,128)(2,1)S(1)}, u32[]{:S(2)}, u32[]{:S(2)}) %all-to-all-start) | async-done | bytes 2097184 | tf_op jit(solution)/shard_map/all_to_all | solution.py:99
  70.4 1.5 %copy.224 = bf16[2,16,128,256]{3,2,1,0:T(8,128)(2,1)} copy(bf16[2,16,128,256]{3,2,0,1:T(8,128)(2,1)S(1)} %all-to-all-done) | data formatting | bytes 4194304 | tf_op jit(solution)/shard_map/all_to_all | solution.py:99
  71.9 29.8 %while.13 = (s32[]{:T(128)}, bf16[2,512,256]{1,2,0:T(8,128)(2,1)}, s32[2]{0:T(128)S(1)}, bf16[2,512,256]{1,2,0:T(8,128)(2,1)S(1)}, bf16[512,512]{0,1:T(8,128)(2,...) while((s32[]{:T(128)}, bf16[2,512,256]{1,2,0:T(8,128)(2,1)}, ...), condition=%wide.region_8.9_spmd.clone, body=%wide.region_3.8_spmd.clone.sunk | while | flops 1369569280 | bytes 69800768 | solution.py:127
  73.9 2.4 %bitcast_reduce_fusion.2 = (f32[512,2]{0,1:T(2,128)S(1)}, f32[2048,512,2]{1,0,2:T(8,128)S(1)}) fusion(pred[2048]{0:T(1024)(128)(4,1)S(1)} %broadcast_bitcast_fusion.2, bf16[512,2,128]{0,2,1:T(8,128)(2,1)S(1)} %bitcast.255, bf16[2,2048,256]{2,1,0:T(8,128)(2,1)} %get-tuple-element.258, s32[]{:T(128)S(6)} %select_n.523), kind=kOutput, calls=%fused_computation.9.clone.1 | convolution fusion | flops 543161344 | bytes 9181188 | tf_op jit(solution)/shard_map/while/body/eval_jaxpr/tkgd,nkd->tkgn/dot_general | solution.py:47
  77.0 1.9 %fusion.63 = f32[512,2]{0,1:T(2,128)S(1)} fusion(f32[2048,512,2]{1,0,2:T(8,128)S(1)} %get-tuple-element.221, f32[512,2]{0,1:T(2,128)S(1)} %max.38, pred[2048]{0:T(1024)(128)(4,1)S(1)} %broadcast_bitcast_fusion.2), kind=kLoop, calls=%fused_computation.12.clone.1 | loop fusion | flops 8387584 | bytes 8398848 | tf_op jit(solution)/shard_map/while/body/eval_jaxpr/reduce_sum | solution.py:55
  79.9 5.7 %fusion.61 = f32[128,512,2]{1,0,2:T(8,128)S(1)} fusion(f32[2048,512,2]{1,0,2:T(8,128)} %copy-done.1, f32[512,2]{0,1:T(2,128)S(1)} %max.38, pred[2048]{0:T(1024)(128)(4,1)S(1)} %broadcast_bitcast_fusion.2, bf16[2,2048,256]{2,1,0:T(8,128)(2,1)} %get-tuple-element.258, s32[]{:T(128)S(6)} %add.121, s32[]{:T(128)S(6)} %select_n.523), kind=kOutput, calls=%fused_computation.15.clone.1 | convolution fusion | flops 545259520 | bytes 9443336 | tf_op jit(solution)/shard_map/while/body/eval_jaxpr/tkgn,nkd->tkgd/dot_general | solution.py:62
  88.8 2.4 %bitcast_reduce_fusion.2 = (f32[512,2]{0,1:T(2,128)S(1)}, f32[2048,512,2]{1,0,2:T(8,128)S(1)}) fusion(pred[2048]{0:T(1024)(128)(4,1)S(1)} %broadcast_bitcast_fusion.2, bf16[512,2,128]{0,2,1:T(8,128)(2,1)S(1)} %bitcast.255, bf16[2,2048,256]{2,1,0:T(8,128)(2,1)} %get-tuple-element.258, s32[]{:T(128)S(6)} %select_n.523), kind=kOutput, calls=%fused_computation.9.clone.1 | convolution fusion | flops 543161344 | bytes 9181188 | tf_op jit(solution)/shard_map/while/body/eval_jaxpr/tkgd,nkd->tkgn/dot_general | solution.py:47
  91.9 1.9 %fusion.63 = f32[512,2]{0,1:T(2,128)S(1)} fusion(f32[2048,512,2]{1,0,2:T(8,128)S(1)} %get-tuple-element.221, f32[512,2]{0,1:T(2,128)S(1)} %max.38, pred[2048]{0:T(1024)(128)(4,1)S(1)} %broadcast_bitcast_fusion.2), kind=kLoop, calls=%fused_computation.12.clone.1 | loop fusion | flops 8387584 | bytes 8398848 | tf_op jit(solution)/shard_map/while/body/eval_jaxpr/reduce_sum | solution.py:55
  94.8 5.7 %fusion.61 = f32[128,512,2]{1,0,2:T(8,128)S(1)} fusion(f32[2048,512,2]{1,0,2:T(8,128)} %copy-done.1, f32[512,2]{0,1:T(2,128)S(1)} %max.38, pred[2048]{0:T(1024)(128)(4,1)S(1)} %broadcast_bitcast_fusion.2, bf16[2,2048,256]{2,1,0:T(8,128)(2,1)} %get-tuple-element.258, s32[]{:T(128)S(6)} %add.121, s32[]{:T(128)S(6)} %select_n.523), kind=kOutput, calls=%fused_computation.15.clone.1 | convolution fusion | flops 545259520 | bytes 9443336 | tf_op jit(solution)/shard_map/while/body/eval_jaxpr/tkgn,nkd->tkgd/dot_general | solution.py:62
  101.7 1.2 %reshape.412 = bf16[2,2,128,512]{2,1,0,3:T(2,128)(2,1)S(1)} reshape(bf16[512,2,256]{0,2,1:T(8,128)(2,1)} %bitcast.35) | data formatting | bytes 1048576 | tf_op jit(solution)/shard_map/reshape;reshape | solution.py:131
  105.1 1.5 %collective-permute-done.4 = bf16[2,128,512]{2,1,0:T(8,128)(2,1)S(1)} collective-permute-done((bf16[2,128,512]{2,1,0:T(8,128)(2,1)S(1)}, bf16[2,128,512]{2,1,0:T(8,128)(2,1)S(1)}, u32[]{:S(2)}, u32[]{:S(2)}) %collective-permute-start.4) | collective-permute-done | bytes 262176 | tf_op jit(solution)/shard_map/ppermute | solution.py:16
  106.9 8.3 %collective-permute-done.5 = bf16[1,128,1024]{2,1,0:T(8,128)(2,1)S(1)} collective-permute-done((bf16[1,128,1024]{2,1,0:T(8,128)(2,1)S(1)}, bf16[1,128,1024]{2,1,0:T(8,128)(2,1)S(1)}, u32[]{:S(2)}, u32[]{:S(2)}) %collective-permute-start.5) | collective-permute-done | bytes 262176 | tf_op jit(solution)/shard_map/ppermute | solution.py:16
  115.3 0.8 maximum_bitcast_fusion.1
  (90 shorter events, 20.5 us)
Async XLA Ops:
  0.0 0.7 copy-start
  16.5 6.3 %copy-start.2 = (bf16[128,2048]{1,0:T(8,128)(2,1)S(1)}, bf16[128,2048]{1,0:T(8,128)(2,1)}, u32[]{:S(2)}) copy-start(bf16[128,2048]{1,0:T(8,128)(2,1)} %param.9) | copy-start | bytes 1572868
  16.5 53.9 %all-to-all-start = ((bf16[2,16,128,256]{3,2,0,1:T(8,128)(2,1)}), bf16[2,16,128,256]{3,2,0,1:T(8,128)(2,1)S(1)}, u32[]{:S(2)}, u32[]{:S(2)}) async-start(bf16[2,16,128,256]{3,2,0,1:T(8,128)(2,1)} %copy.223), calls=%async_computation | async-start | bytes 4194304 | tf_op jit(solution)/shard_map/all_to_all | solution.py:99
  23.8 3.0 %collective-permute-start.2 = (bf16[128,2,512]{0,2,1:T(8,128)(2,1)}, bf16[128,2,512]{0,2,1:T(8,128)(2,1)}, u32[]{:S(2)}, u32[]{:S(2)}) collective-permute-start(bf16[128,2,512]{0,2,1:T(8,128)(2,1)} %fusion.32), channel_id=1, source_target_pairs={{0,1},{1,0},{2,3},{3,2},{4,5},{5,4},{6,7},{7,6},{8,9},{9,8},{10,11... | collective-permute-start | bytes 786440 | tf_op jit(solution)/shard_map/ppermute | solution.py:16
  26.0 3.4 %collective-permute-start = (bf16[2,128,2,256]{1,3,2,0:T(8,128)(2,1)}, bf16[2,128,2,256]{1,3,2,0:T(8,128)(2,1)S(1)}, u32[]{:S(2)}, u32[]{:S(2)}) collective-permute-start(bf16[2,128,2,256]{1,3,2,0:T(8,128)(2,1)} %fusion.34), channel_id=1, source_target_pairs={{0,1},{1,0},{2,3},{3,2},{4,5},{5,4},{6,7},{7,6},{8,9},{9,8},{10,11... | collective-permute-start | bytes 786440 | tf_op jit(solution)/shard_map/ppermute | solution.py:16
  27.9 15.8 %collective-permute-start.3 = (bf16[256,512]{0,1:T(8,128)(2,1)S(1)}, bf16[256,512]{0,1:T(8,128)(2,1)S(1)}, u32[]{:S(2)}, u32[]{:S(2)}) collective-permute-start(bf16[256,512]{0,1:T(8,128)(2,1)S(1)} %select_bitcast_fusion.2), channel_id=1, source_target_pairs={{0,2},{1,3},{2,0},{3,1},{4,6},{5,7},{6,4},{7,5},{8,10},{9,11},{10,... | collective-permute-start | bytes 786440 | tf_op jit(solution)/shard_map/ppermute | solution.py:16
  29.5 21.7 %collective-permute-start.1 = (bf16[2,256,256]{1,2,0:T(8,128)(2,1)S(1)}, bf16[2,256,256]{1,2,0:T(8,128)(2,1)S(1)}, u32[]{:S(2)}, u32[]{:S(2)}) collective-permute-start(bf16[2,256,256]{1,2,0:T(8,128)(2,1)S(1)} %fusion.33), channel_id=1, source_target_pairs={{0,2},{1,3},{2,0},{3,1},{4,6},{5,7},{6,4},{7,5},{8,10},{9,11},{10,... | collective-permute-start | bytes 786440 | tf_op jit(solution)/shard_map/ppermute | solution.py:16
  76.3 3.2 %copy-start.1 = (f32[2048,512,2]{1,0,2:T(8,128)}, f32[2048,512,2]{1,0,2:T(8,128)S(1)}, u32[]{:S(2)}) copy-start(f32[2048,512,2]{1,0,2:T(8,128)S(1)} %get-tuple-element.221) | copy-start | bytes 25165828 | tf_op jit(solution)/shard_map/while
  91.3 3.2 %copy-start.1 = (f32[2048,512,2]{1,0,2:T(8,128)}, f32[2048,512,2]{1,0,2:T(8,128)S(1)}, u32[]{:S(2)}) copy-start(f32[2048,512,2]{1,0,2:T(8,128)S(1)} %get-tuple-element.221) | copy-start | bytes 25165828 | tf_op jit(solution)/shard_map/while
  105.1 1.6 %collective-permute-start.4 = (bf16[2,128,512]{2,1,0:T(8,128)(2,1)S(1)}, bf16[2,128,512]{2,1,0:T(8,128)(2,1)S(1)}, u32[]{:S(2)}, u32[]{:S(2)}) collective-permute-start(bf16[2,128,512]{2,1,0:T(8,128)(2,1)S(1)} %fusion.35), channel_id=1, source_target_pairs={{0,1},{1,0},{2,3},{3,2},{4,5},{5,4},{6,7},{7,6},{8,9},{9,8},{10,11... | collective-permute-start | bytes 786440 | tf_op jit(solution)/shard_map/ppermute | solution.py:16
  106.8 8.4 %collective-permute-start.5 = (bf16[1,128,1024]{2,1,0:T(8,128)(2,1)S(1)}, bf16[1,128,1024]{2,1,0:T(8,128)(2,1)S(1)}, u32[]{:S(2)}, u32[]{:S(2)}) collective-permute-start(bf16[1,128,1024]{2,1,0:T(8,128)(2,1)S(1)} %select_bitcast_fusion.1), channel_id=1, source_target_pairs={{0,2},{1,3},{2,0},{3,1},{4,6},{5,7},{6,4},{7,5},{8,10},{9,11},{10,... | collective-permute-start | bytes 786440 | tf_op jit(solution)/shard_map/ppermute | solution.py:16
where the time goes:
time: 117 us; the launch traced here: 116 us
  waiting for transfers between devices  49.7 us (42%)
  local copies, waits for them, and re-layouts  24.3 us (21%)
  matrix products  18.4 us (16%)
  other arithmetic  11.8 us (10%)
  starting transfers between devices  9.1 us (8%)
  loops' own time  2.68 us (2%)
    ppermute x6, waiting for transfers between devices, swapped(): lax.ppermute(x, axis, [(i, i ^ 1 << distance) for i in range(lax.axis_siz...  30.7 us
    all_to_all x1, waiting for transfers between devices, local(): lax.all_to_all(sending, 'nodes', split_axis=1, concat_axis=1, tiled=True)  19 us
    dot_general x2, matrix products, attend_core(): jnp.einsum('tkgn,nkd->tkgd', anc_weights.astype(jnp.bfloat16), anc_block[...  11.4 us
    all_to_all x1, starting transfers between devices, local(): lax.all_to_all(sending, 'nodes', split_axis=1, concat_axis=1, tiled=True)  6.29 us
    gather x1, local copies, waits for them, and re-layouts, local(): picked = jnp.take(kv_store, slot_pick, axis=1)  5.71 us
    dot_general x2, matrix products, attend_core(): jnp.einsum('tkgd,nkd->tkgn', query_block, anc_block[0], preferred_element...  4.81 us
    unnamed x10, local copies, waits for them, and re-layouts  4.48 us
    reduce_sum x4, other arithmetic, attend_core(): weight_sum = jnp.sum(own_weights, axis=-1) + jnp.sum(anc_weights, axis=-1)  4.32 us
  transfers between devices with their start and end apart: 7, of which 5 were waited for; matrix products, arithmetic and copies ran while one was open for 4% of the time, Pallas kernels for 0%

commit v1 on v0

v1 whole, which is shorter than its diff:
```python
import jax
import jax.numpy as jnp
from jax import lax
from jax.experimental import pallas as pl
from jax.experimental.pallas import tpu as pltpu
from jax.sharding import PartitionSpec as P

HEADS = 16
KV_HEADS = 8
HEAD_DIM = 128
DEPTHS = 4
MEMBERS = 4
GROUP = HEADS // KV_HEADS

query_scale = 168.0 ** (-0.5)
exp2_scale = query_scale * 1.4426950408889634


def dot_t(a, b):
    return lax.dot_general(a, b, (((1,), (1,)), ((), ())), preferred_element_type=jnp.float32)


def dot(a, b):
    return lax.dot_general(a, b, (((1,), (0,)), ((), ())), preferred_element_type=jnp.float32)


def stage_kernel(parent, up, owner, slot, queries, seg_kv, store, *rest):
    send, p0, p1, p2, p3, bias = rest[:6]
    late, (picks, sems) = rest[6:-2], rest[-2:]
    me = lax.axis_index("nodes")
    member = me % MEMBERS
    segment = me // MEMBERS
    segs = parent.shape[0]
    blocks, pages = owner.shape
    q_cols = queries.shape[1] // MEMBERS
    kv_cols = seg_kv.shape[2] // MEMBERS

    def path_rows(g):
        rows = lax.broadcasted_iota(jnp.int32, (blocks, 1), 0)
        current = parent[g]
        on_path = rows == current
        for _ in range(DEPTHS - 1):
            current = jnp.where(current >= 0, up[jnp.maximum(current, 0)], -1)
            on_path = on_path | (rows == current)
        return on_path

    held = owner[...] == me
    pick_of = jnp.max(jnp.where(held, slot[...], 0), axis=1, keepdims=True)

    def one_segment(g, carry):
        pick = jnp.max(jnp.where(path_rows(g), pick_of, 0))
        picks[g] = pick
        for m in range(MEMBERS):
            to = g * MEMBERS + m
            col = m * kv_cols
            pltpu.make_async_copy(
                store.at[0, pick, :, pl.ds(col, HEAD_DIM)], send.at[to, 0], sems.at[4]
            ).start()
            pltpu.make_async_copy(
                store.at[0, pick, :, pl.ds(col + HEAD_DIM, HEAD_DIM)], send.at[to, 1], sems.at[4]
            ).start()
            pltpu.make_async_copy(
                store.at[1, pick, :, pl.ds(col, HEAD_DIM)], send.at[to, 2], sems.at[4]
            ).start()
        return carry

    lax.fori_loop(0, segs, one_segment, 0, unroll=segs <= 4)
    for d, ref in enumerate(late):
        to = me ^ d
        col = pl.multiple_of(to % MEMBERS * kv_cols, kv_cols) + HEAD_DIM
        pltpu.make_async_copy(
            store.at[1, picks[to // MEMBERS], :, pl.ds(pl.multiple_of(col, HEAD_DIM), HEAD_DIM)], ref, sems.at[5 + d]
        ).start()
    for d, piece in enumerate((p0, p1, p2, p3)):
        to = member ^ d
        q_at = pl.multiple_of(to * q_cols, q_cols)
        kv_at = pl.multiple_of(to * kv_cols, kv_cols)
        pltpu.make_async_copy(queries.at[:, pl.ds(q_at, q_cols)], piece.at[:, pl.ds(0, q_cols)], sems.at[d]).start()
        for i in range(2):
            pltpu.make_async_copy(
                seg_kv.at[i, :, pl.ds(kv_at, kv_cols)],
                piece.at[:, pl.ds(q_cols + i * kv_cols, kv_cols)],
                sems.at[d],
            ).start()
    page_tok = store.shape[2]
    mine = path_rows(segment)
    for at in range(0, bias.shape[1], 128):
        page = (lax.broadcasted_iota(jnp.int32, (blocks, 128), 1) + at) // page_tok
        found = jnp.zeros((blocks, 128), jnp.float32)
        for p in range(pages):
            found = jnp.where(mine & (owner[:, p : p + 1] == page), 1.0, found)
        found = jnp.max(found, axis=0, keepdims=True)
        bias[:, at : at + 128] = jnp.where(found > 0.0, 0.0, -jnp.inf)
    for i, ref in enumerate((p0, p1, p2, p3, send, *late)):
        pltpu.make_async_copy(ref, ref, sems.at[i]).wait()


def head_inputs(pieces, h, q_cols, kv_cols):
    q, k, v = [], [], []
    for piece in pieces:
        at = h * GROUP * HEAD_DIM
        q.append([piece[:, at + i * HEAD_DIM : at + (i + 1) * HEAD_DIM] for i in range(GROUP)])
        at = q_cols + h * HEAD_DIM
        k.append(piece[:, at : at + HEAD_DIM])
        v.append(piece[:, at + kv_cols : at + kv_cols + HEAD_DIM])
    queries = [jnp.concatenate(one, axis=0) for one in q]
    return queries, jnp.concatenate(k, axis=0), jnp.concatenate(v, axis=0)


def own_mask(member, d, rows, tok):
    cols = MEMBERS * tok
    r = lax.broadcasted_iota(jnp.int32, (rows, cols), 0)
    c = lax.broadcasted_iota(jnp.int32, (rows, cols), 1)
    q_at = (member ^ d) * tok + r % tok
    k_at = (member ^ (c // tok)) * tok + c % tok
    return k_at <= q_at


def softmax_parts(q, k_own, k_pages, bias_ref, score_ref, visible, step):
    keys = k_pages.shape[0]
    own = jnp.where(visible, dot_t(q, k_own), -jnp.inf)
    top = jnp.max(own, axis=1, keepdims=True)
    for at in range(0, keys, step):
        s = dot_t(q, k_pages[at : at + step]) + bias_ref[:, at : at + step]
        score_ref[:, at : at + step] = s
        top = jnp.maximum(top, jnp.max(s, axis=1, keepdims=True))
    top = top * exp2_scale
    own = jnp.exp2(own * exp2_scale - top)
    return own, top


def full_kernel(page_tok, h, bias_ref, p0, p1, p2, p3, pages, o0, o1, o2, o3, score_ref):
    member = lax.axis_index("nodes") % MEMBERS
    tok = p0.shape[0]
    q_cols = p0.shape[1] // 2
    kv_cols = q_cols // GROUP
    queries, k_own, v_own = head_inputs((p0, p1, p2, p3), h, q_cols, kv_cols)
    keys = pages.shape[0] * page_tok
    step = min(keys, 512)
    k_pages = pages[:, 0].reshape(keys, HEAD_DIM)
    for d, out in enumerate((o0, o1, o2, o3)):
        visible = own_mask(member, d, GROUP * tok, tok)
        own, top = softmax_parts(queries[d], k_own, k_pages, bias_ref, score_ref, visible, step)
        total = jnp.sum(own, axis=1, keepdims=True)
        mixed = dot(own.astype(jnp.bfloat16), v_own)
        for at in range(0, keys, step):
            w = jnp.exp2(score_ref[:, at : at + step] * exp2_scale - top)
            total = total + jnp.sum(w, axis=1, keepdims=True)
            v = pages[at // page_tok : (at + step) // page_tok, 2].reshape(step, HEAD_DIM)
            mixed = mixed + dot(w.astype(jnp.bfloat16), v)
        res = (mixed / total).astype(jnp.bfloat16)
        for i in range(GROUP):
            out[:, i * HEAD_DIM : (i + 1) * HEAD_DIM] = res[i * tok : (i + 1) * tok]


def weights_kernel(page_tok, h, bias_ref, p0, p1, p2, p3, pages, w_ref, mixed_ref, total_ref, score_ref):
    member = lax.axis_index("nodes") % MEMBERS
    tok = p0.shape[0]
    q_cols = p0.shape[1] // 2
    kv_cols = q_cols // GROUP
    queries, k_own, v_own = head_inputs((p0, p1, p2, p3), h, q_cols, kv_cols)
    keys = pages.shape[0] * page_tok
    step = min(keys, 512)
    k_pages = pages[:, 1].reshape(keys, HEAD_DIM)
    for d in range(MEMBERS):
        visible = own_mask(member, d, GROUP * tok, tok)
        own, top = softmax_parts(queries[d], k_own, k_pages, bias_ref, score_ref, visible, step)
        total = jnp.sum(own, axis=1, keepdims=True)
        mixed_ref[d] = dot(own.astype(jnp.bfloat16), v_own)
        for at in range(0, keys, step):
            w = jnp.exp2(score_ref[:, at : at + step] * exp2_scale - top)
            total = total + jnp.sum(w, axis=1, keepdims=True)
            w_ref[d, :, at : at + step] = w.astype(jnp.bfloat16)
        total_ref[d] = jnp.broadcast_to(total, total_ref.shape[1:])


def values_kernel(w_ref, mixed_ref, total_ref, *rest):
    late, outs, v_ref = rest[: -MEMBERS - 1], rest[-MEMBERS - 1 : -1], rest[-1]
    me = lax.axis_index("nodes")
    tok = outs[0].shape[0]
    page_tok = late[0].shape[0]
    for d, ref in enumerate(late):
        v_ref[pl.ds(pl.multiple_of((me ^ d) * page_tok, page_tok), page_tok)] = ref[...]
    for d, out in enumerate(outs):
        mixed = mixed_ref[d] + dot(w_ref[d], v_ref[...])
        res = (mixed / total_ref[d]).astype(jnp.bfloat16)
        for i in range(GROUP):
            out[:, i * HEAD_DIM : (i + 1) * HEAD_DIM] = res[i * tok : (i + 1) * tok]


def join_kernel(*refs):
    parts, out, sems = refs[:8], refs[8], refs[9]
    member = lax.axis_index("nodes") % MEMBERS
    width = parts[0].shape[1]
    copies = []
    for h in range(2):
        for d in range(MEMBERS):
            at = pl.multiple_of(((member ^ d) * 2 + h) * width, width)
            i = h * MEMBERS + d
            copies.append(pltpu.make_async_copy(parts[i], out.at[:, pl.ds(at, width)], sems.at[i]))
    for c in copies:
        c.start()
    for c in copies:
        c.wait()


def local(queries, seg_kv, kv_store, seg_parent, block_up, page_owner, page_slot):
    nodes = lax.axis_size("nodes")
    tok = queries.shape[0]
    page_tok = kv_store.shape[2]
    keys = nodes * page_tok
    bf16, f32 = jnp.bfloat16, jnp.float32
    any_spec = pl.BlockSpec(memory_space=pl.ANY)
    smem = pl.BlockSpec(memory_space=pltpu.SMEM)
    vmem = pl.BlockSpec(memory_space=pltpu.VMEM)
    params = pltpu.CompilerParams(vmem_limit_bytes=24 * 2**20)
    piece = jax.ShapeDtypeStruct((tok, queries.shape[1] // MEMBERS + 2 * seg_kv.shape[2] // MEMBERS), bf16)
    late = jax.ShapeDtypeStruct((page_tok, HEAD_DIM), bf16)
    early = jax.ShapeDtypeStruct((nodes, 3, page_tok, HEAD_DIM), bf16)
    staged = pl.pallas_call(
        stage_kernel,
        in_specs=[smem] * 2 + [vmem] * 2 + [any_spec] * 3,
        out_specs=[vmem] * (6 + nodes),
        out_shape=[early, *[piece] * MEMBERS, jax.ShapeDtypeStruct((1, keys), f32), *[late] * nodes],
        scratch_shapes=[pltpu.SMEM((nodes // MEMBERS,), jnp.int32), pltpu.SemaphoreType.DMA((5 + nodes,))],
        compiler_params=params,
        name="stage",
    )(seg_parent, block_up, page_owner, page_slot, queries, seg_kv, kv_store)
    send, p0, p1, p2, p3, bias = staged[:6]
    held = staged[6:]

    def exchange(x):
        return lax.all_to_all(x, "nodes", split_axis=0, concat_axis=0, tiled=True)

    def swapped(x, d):
        return lax.ppermute(x, "nodes", [(i, i ^ d) for i in range(nodes)])

    got = exchange(send)
    pieces = (p0, swapped(p1, 1), swapped(p2, 2), swapped(p3, 3))
    values = [held[0]] + [swapped(held[d], d) for d in range(1, nodes)]
    rows = GROUP * tok
    scratch = [pltpu.VMEM((rows, keys), f32)]
    out_piece = jax.ShapeDtypeStruct((tok, GROUP * HEAD_DIM), bf16)
    out_a = pl.pallas_call(
        lambda *refs: full_kernel(page_tok, 0, *refs),
        in_specs=[vmem] * 6,
        out_specs=[vmem] * 4,
        out_shape=[out_piece] * 4,
        scratch_shapes=scratch,
        compiler_params=params,
        name="full",
    )(bias, *pieces, got)
    weights, mixed, total = pl.pallas_call(
        lambda *refs: weights_kernel(page_tok, 1, *refs),
        in_specs=[vmem] * 6,
        out_specs=[vmem] * 3,
        out_shape=[
            jax.ShapeDtypeStruct((MEMBERS, rows, keys), bf16),
            jax.ShapeDtypeStruct((MEMBERS, rows, HEAD_DIM), f32),
            jax.ShapeDtypeStruct((MEMBERS, rows, HEAD_DIM), f32),
        ],
        scratch_shapes=scratch,
        compiler_params=params,
        name="weights",
    )(bias, *pieces, got)
    out_b = pl.pallas_call(
        values_kernel,
        in_specs=[vmem] * (3 + nodes),
        out_specs=[vmem] * 4,
        out_shape=[out_piece] * 4,
        scratch_shapes=[pltpu.VMEM((keys, HEAD_DIM), bf16)],
        compiler_params=params,
        name="values",
    )(weights, mixed, total, *values)
    parts = []
    for one in (out_a, out_b):
        parts += [one[0]] + [swapped(one[d], d) for d in range(1, MEMBERS)]
    return pl.pallas_call(
        join_kernel,
        in_specs=[vmem] * 8,
        out_specs=any_spec,
        out_shape=jax.ShapeDtypeStruct(queries.shape, bf16),
        scratch_shapes=[pltpu.SemaphoreType.DMA((8,))],
        compiler_params=params,
        name="join",
    )(*parts)


def solution(mesh):
    in_specs = (
        P(("groups", "nodes"), None),
        P(None, ("groups", "nodes"), None),
        P(None, ("groups", "nodes"), None, None),
        P("groups"),
        P("groups"),
        P("groups", None),
        P("groups", None),
    )
    out_specs = P(("groups", "nodes"), None)

    return jax.shard_map(local, mesh=mesh, in_specs=in_specs, out_specs=out_specs, check_vma=False)
```

time: 117 us -> 99 us (0.85)
  the two profiles are of different devices: /device:TPU:16 before, /device:TPU:0 now
where the time goes in v1:
time: 99 us; the launch traced here: 98.6 us
  starting transfers between devices  38.4 us (39%)
  waiting for transfers between devices  32.6 us (33%)
  Pallas kernels  14 us (14%)
  local copies, waits for them, and re-layouts  13.6 us (14%)
    ppermute x24, waiting for transfers between devices, swapped(): return lax.ppermute(x, 'nodes', [(i, i ^ d) for i in range(nodes)])  32.6 us
    ppermute x24, starting transfers between devices, swapped(): return lax.ppermute(x, 'nodes', [(i, i ^ d) for i in range(nodes)])  31 us
    unnamed x30, local copies, waits for them, and re-layouts  13.6 us
    all_to_all x1, starting transfers between devices, exchange(): return lax.all_to_all(x, 'nodes', split_axis=0, concat_axis=0, tiled=True)  7.39 us
    pallas_call x1, Pallas kernels, local(): pl.pallas_call(lambda *refs: full_kernel(page_tok, 0, *refs), in_specs=[v...  4.38 us
    pallas_call x1, Pallas kernels, local(): pl.pallas_call(stage_kernel, in_specs=[smem] * 2 + [vmem] * 2 + [any_spec...  3.92 us
    pallas_call x1, Pallas kernels, local(): pl.pallas_call(lambda *refs: weights_kernel(page_tok, 1, *refs), in_specs...  3.53 us
  transfers between devices with their start and end apart: 25, of which 6 were waited for; matrix products, arithmetic and copies ran while one was open for 0% of the time, Pallas kernels for 9%

profile of v1, /device:TPU:0, one launch (start us, length us, event | category | flops | bytes accessed | tf_op | source)
XLA Modules:
  0.0 98.6 jit_solution(3365881980297864498)
XLA Ops:
  1.5 5.0 %copy-done = bf16[2,27,128,1024]{3,2,1,0:T(8,128)(2,1)S(1)} copy-done((bf16[2,27,128,1024]{3,2,1,0:T(8,128)(2,1)S(1)}, bf16[2,27,128,1024]{3,2,1,0:T(8,128)(2,1)}, u32[]{:S(2)}) %copy-start) | copy-done | bytes 14155800
  6.6 1.0 %copy-done.1 = bf16[128,2048]{1,0:T(8,128)(2,1)S(1)} copy-done((bf16[128,2048]{1,0:T(8,128)(2,1)S(1)}, bf16[128,2048]{1,0:T(8,128)(2,1)}, u32[]{:S(2)}) %copy-start.1) | copy-done | bytes 524312
  7.6 1.0 %copy-done.2 = bf16[2,128,1024]{2,1,0:T(8,128)(2,1)S(1)} copy-done((bf16[2,128,1024]{2,1,0:T(8,128)(2,1)S(1)}, bf16[2,128,1024]{2,1,0:T(8,128)(2,1)}, u32[]{:S(2)}) %copy-start.2) | copy-done | bytes 524312
  9.9 3.9 %stage.1 = (bf16[16,3,128,128]{3,2,1,0:T(8,128)(2,1)}, bf16[128,1024]{1,0:T(8,128)(2,1)S(1)}, bf16[128,1024]{1,0:T(8,128)(2,1)}, bf16[128,1024]{1,0:T(8,128)(2,1...) custom-call(s32[4]{0:T(128)S(1)} %copy-done.3, ...), custom_call_target="tpu_custom_call" | custom-call | tf_op jit(solution)/shard_map/stage/pallas_call | solution.py:220
  17.5 7.4 %all-to-all-start = ((bf16[16,3,128,128]{3,2,1,0:T(8,128)(2,1)}), bf16[16,3,128,128]{3,2,1,0:T(8,128)(2,1)S(1)}, u32[]{:S(2)}, u32[]{:S(2)}) async-start(bf16[16,3,128,128]{3,2,1,0:T(8,128)(2,1)} %get-tuple-element.43), calls=%async_computation | async-start | bytes 3145728 | tf_op jit(solution)/shard_map/all_to_all | solution.py:233
  25.3 1.6 %collective-permute-start.1 = (bf16[128,1024]{1,0:T(8,128)(2,1)S(1)}, bf16[128,1024]{1,0:T(8,128)(2,1)S(1)}, u32[]{:S(2)}, u32[]{:S(2)}) collective-permute-start(bf16[128,1024]{1,0:T(8,128)(2,1)S(1)} %get-tuple-element.41), channel_id=1, source_target_pairs={{0,2},{1,3},{2,0},{3,1},{4,6},{5,7},{6,4},{7,5},{8,10},{9,11},{10,... | collective-permute-start | bytes 786440 | tf_op jit(solution)/shard_map/ppermute | solution.py:236
  27.5 1.6 %collective-permute-start.7 = (bf16[128,128]{1,0:T(8,128)(2,1)}, bf16[128,128]{1,0:T(8,128)(2,1)S(1)}, u32[]{:S(2)}, u32[]{:S(2)}) collective-permute-start(bf16[128,128]{1,0:T(8,128)(2,1)} %copy-done.12), channel_id=1, source_target_pairs={{0,2},{1,3},{2,0},{3,1},{4,6},{5,7},{6,4},{7,5},{8,10},{9,11},{10,... | collective-permute-start | bytes 98312 | tf_op jit(solution)/shard_map/ppermute | solution.py:236
  30.2 23.1 %collective-permute-done.7.rest_2_ = bf16[128,128]{1,0:T(8,128)(2,1)S(1)} collective-permute-done((bf16[128,128]{1,0:T(8,128)(2,1)}, bf16[128,128]{1,0:T(8,128)(2,1)S(1)}, u32[]{:S(2)}, u32[]{:S(2)}) %collective-permute-start.7) | collective-permute-done | bytes 32800 | tf_op jit(solution)/shard_map/ppermute | solution.py:236
  53.3 3.2 %collective-permute-start.9 = (bf16[128,128]{1,0:T(8,128)(2,1)}, bf16[128,128]{1,0:T(8,128)(2,1)S(1)}, u32[]{:S(2)}, u32[]{:S(2)}) collective-permute-start(bf16[128,128]{1,0:T(8,128)(2,1)} %get-tuple-element.55), channel_id=1, source_target_pairs={{0,4},{1,5},{2,6},{3,7},{4,0},{5,1},{6,2},{7,3},{8,12},{9,13},{10,... | collective-permute-start | bytes 98312 | tf_op jit(solution)/shard_map/ppermute | solution.py:236
  56.5 2.6 %collective-permute-done.9.rest_4_ = bf16[128,128]{1,0:T(8,128)(2,1)S(1)} collective-permute-done((bf16[128,128]{1,0:T(8,128)(2,1)}, bf16[128,128]{1,0:T(8,128)(2,1)S(1)}, u32[]{:S(2)}, u32[]{:S(2)}) %collective-permute-start.9) | collective-permute-done | bytes 32800 | tf_op jit(solution)/shard_map/ppermute | solution.py:236
  59.1 1.5 %collective-permute-start.11 = (bf16[128,128]{1,0:T(8,128)(2,1)}, bf16[128,128]{1,0:T(8,128)(2,1)S(1)}, u32[]{:S(2)}, u32[]{:S(2)}) collective-permute-start(bf16[128,128]{1,0:T(8,128)(2,1)} %get-tuple-element.57), channel_id=1, source_target_pairs={{0,6},{1,7},{2,4},{3,5},{4,2},{5,3},{6,0},{7,1},{8,14},{9,15},{10,... | collective-permute-start | bytes 98312 | tf_op jit(solution)/shard_map/ppermute | solution.py:236
  61.3 2.9 %collective-permute-done.11.rest_6_ = bf16[128,128]{1,0:T(8,128)(2,1)S(1)} collective-permute-done((bf16[128,128]{1,0:T(8,128)(2,1)}, bf16[128,128]{1,0:T(8,128)(2,1)S(1)}, u32[]{:S(2)}, u32[]{:S(2)}) %collective-permute-start.11) | collective-permute-done | bytes 32800 | tf_op jit(solution)/shard_map/ppermute | solution.py:236
  64.2 4.0 %collective-permute-start.13 = (bf16[128,128]{1,0:T(8,128)(2,1)}, bf16[128,128]{1,0:T(8,128)(2,1)S(1)}, u32[]{:S(2)}, u32[]{:S(2)}) collective-permute-start(bf16[128,128]{1,0:T(8,128)(2,1)} %copy-done.10), channel_id=1, source_target_pairs={{0,8},{1,9},{2,10},{3,11},{4,12},{5,13},{6,14},{7,15},{8,0},{9,1},... | collective-permute-start | bytes 98312 | tf_op jit(solution)/shard_map/ppermute | solution.py:236
  68.8 2.6 %collective-permute-start.16 = (bf16[128,128]{1,0:T(8,128)(2,1)}, bf16[128,128]{1,0:T(8,128)(2,1)S(1)}, u32[]{:S(2)}, u32[]{:S(2)}) collective-permute-start(bf16[128,128]{1,0:T(8,128)(2,1)} %copy-done.7), channel_id=1, source_target_pairs={{0,11},{1,10},{2,9},{3,8},{4,15},{5,14},{6,13},{7,12},{8,3},{9,2},... | collective-permute-start | bytes 98312 | tf_op jit(solution)/shard_map/ppermute | solution.py:236
  71.5 4.4 %full.1 = (bf16[128,256]{1,0:T(8,128)(2,1)S(1)}, bf16[128,256]{1,0:T(8,128)(2,1)S(1)}, bf16[128,256]{1,0:T(8,128)(2,1)S(1)}, bf16[128,256]{1,0:T(8,128)(2,1)S(1)}) custom-call(f32[1,2048]{1,0:T(1,128)S(1)} %get-tuple-element.38.refs_0_, bf16[128,1024]{1,0:T(8,128)(2,1)S(1)} %get-tuple-element.39.refs_1_, bf16[128,1024]{1,0:T(8,128)(2,1)S(1)} %collective-permute-done.refs_2_, ...), custom_call_target="tpu_custom_call" | custom-call | tf_op jit(solution)/shard_map/full/pallas_call | solution.py:244
  76.7 4.1 %collective-permute-start.17 = (bf16[128,128]{1,0:T(8,128)(2,1)}, bf16[128,128]{1,0:T(8,128)(2,1)S(1)}, u32[]{:S(2)}, u32[]{:S(2)}) collective-permute-start(bf16[128,128]{1,0:T(8,128)(2,1)} %copy-done.6), channel_id=1, source_target_pairs={{0,12},{1,13},{2,14},{3,15},{4,8},{5,9},{6,10},{7,11},{8,4},{9,5},... | collective-permute-start | bytes 98312 | tf_op jit(solution)/shard_map/ppermute | solution.py:236
  80.8 2.2 %collective-permute-start.19 = (bf16[128,128]{1,0:T(8,128)(2,1)S(1)}, bf16[128,128]{1,0:T(8,128)(2,1)S(1)}, u32[]{:S(2)}, u32[]{:S(2)}) collective-permute-start(bf16[128,128]{1,0:T(8,128)(2,1)S(1)} %get-tuple-element.65), channel_id=1, source_target_pairs={{0,14},{1,15},{2,12},{3,13},{4,10},{5,11},{6,8},{7,9},{8,6},{9,7},... | collective-permute-start | bytes 98312 | tf_op jit(solution)/shard_map/ppermute | solution.py:236
  83.1 1.9 %collective-permute-start.20 = (bf16[128,128]{1,0:T(8,128)(2,1)S(1)}, bf16[128,128]{1,0:T(8,128)(2,1)S(1)}, u32[]{:S(2)}, u32[]{:S(2)}) collective-permute-start(bf16[128,128]{1,0:T(8,128)(2,1)S(1)} %get-tuple-element.66), channel_id=1, source_target_pairs={{0,15},{1,14},{2,13},{3,12},{4,11},{5,10},{6,9},{7,8},{8,7},{9,6},... | collective-permute-start | bytes 98312 | tf_op jit(solution)/shard_map/ppermute | solution.py:236
  85.0 3.5 %weights.1 = (bf16[4,256,2048]{2,1,0:T(8,128)(2,1)S(1)}, f32[4,256,128]{2,1,0:T(8,128)S(1)}, f32[4,256,128]{2,1,0:T(8,128)S(1)}) custom-call(f32[1,2048]{1,0:T(1,128)S(1)} %get-tuple-element.38.refs_0_, bf16[128,1024]{1,0:T(8,128)(2,1)S(1)} %get-tuple-element.39.refs_1_, bf16[128,1024]{1,0:T(8,128)(2,1)S(1)} %collective-permute-done.refs_2_, ...), custom_call_target="tpu_custom_call" | custom-call | tf_op jit(solution)/shard_map/weights/pallas_call | solution.py:253
  89.4 1.2 %collective-permute-start.5 = (bf16[128,256]{1,0:T(8,128)(2,1)S(1)}, bf16[128,256]{1,0:T(8,128)(2,1)S(1)}, u32[]{:S(2)}, u32[]{:S(2)}) collective-permute-start(bf16[128,256]{1,0:T(8,128)(2,1)S(1)} %get-tuple-element.47), channel_id=1, source_target_pairs={{0,3},{1,2},{2,1},{3,0},{4,7},{5,6},{6,5},{7,4},{8,11},{9,10},{10,... | collective-permute-start | bytes 196616 | tf_op jit(solution)/shard_map/ppermute | solution.py:236
  90.7 1.3 %values.1 = (bf16[128,256]{1,0:T(8,128)(2,1)S(1)}, bf16[128,256]{1,0:T(8,128)(2,1)S(1)}, bf16[128,256]{1,0:T(8,128)(2,1)S(1)}, bf16[128,256]{1,0:T(8,128)(2,1)S(1)}) custom-call(bf16[4,256,2048]{2,1,0:T(8,128)(2,1)S(1)} %get-tuple-element.48.w_ref, f32[4,256,128]{2,1,0:T(8,128)S(1)} %get-tuple-element.49.mixed_ref, ...), custom_call_target="tpu_custom_call" | custom-call | tf_op jit(solution)/shard_map/values/pallas_call | solution.py:266
  92.1 1.3 %collective-permute-start.22 = (bf16[128,256]{1,0:T(8,128)(2,1)S(1)}, bf16[128,256]{1,0:T(8,128)(2,1)S(1)}, u32[]{:S(2)}, u32[]{:S(2)}) collective-permute-start(bf16[128,256]{1,0:T(8,128)(2,1)S(1)} %get-tuple-element.69), channel_id=1, source_target_pairs={{0,2},{1,3},{2,0},{3,1},{4,6},{5,7},{6,4},{7,5},{8,10},{9,11},{10,... | collective-permute-start | bytes 196616 | tf_op jit(solution)/shard_map/ppermute | solution.py:236
  94.4 2.3 %collective-permute-done.22.refs_6_ = bf16[128,256]{1,0:T(8,128)(2,1)S(1)} collective-permute-done((bf16[128,256]{1,0:T(8,128)(2,1)S(1)}, bf16[128,256]{1,0:T(8,128)(2,1)S(1)}, u32[]{:S(2)}, u32[]{:S(2)}) %collective-permute-start.22) | collective-permute-done | bytes 65568 | tf_op jit(solution)/shard_map/ppermute | solution.py:236
  96.7 1.1 %collective-permute-done.23.refs_7_ = bf16[128,256]{1,0:T(8,128)(2,1)S(1)} collective-permute-done((bf16[128,256]{1,0:T(8,128)(2,1)S(1)}, bf16[128,256]{1,0:T(8,128)(2,1)S(1)}, u32[]{:S(2)}, u32[]{:S(2)}) %collective-permute-start.23) | collective-permute-done | bytes 65568 | tf_op jit(solution)/shard_map/ppermute | solution.py:236
  (61 shorter events, 13.5 us)
Async XLA Ops:
  17.5 54.0 %all-to-all-start = ((bf16[16,3,128,128]{3,2,1,0:T(8,128)(2,1)}), bf16[16,3,128,128]{3,2,1,0:T(8,128)(2,1)S(1)}, u32[]{:S(2)}, u32[]{:S(2)}) async-start(bf16[16,3,128,128]{3,2,1,0:T(8,128)(2,1)} %get-tuple-element.43), calls=%async_computation | async-start | bytes 3145728 | tf_op jit(solution)/shard_map/all_to_all | solution.py:233
  24.9 43.3 %collective-permute-start = (bf16[128,1024]{1,0:T(8,128)(2,1)}, bf16[128,1024]{1,0:T(8,128)(2,1)S(1)}, u32[]{:S(2)}, u32[]{:S(2)}) collective-permute-start(bf16[128,1024]{1,0:T(8,128)(2,1)} %get-tuple-element.40), channel_id=1, source_target_pairs={{0,1},{1,0},{2,3},{3,2},{4,5},{5,4},{6,7},{7,6},{8,9},{9,8},{10,11... | collective-permute-start | bytes 786440 | tf_op jit(solution)/shard_map/ppermute | solution.py:236
  25.3 42.9 %collective-permute-start.1 = (bf16[128,1024]{1,0:T(8,128)(2,1)S(1)}, bf16[128,1024]{1,0:T(8,128)(2,1)S(1)}, u32[]{:S(2)}, u32[]{:S(2)}) collective-permute-start(bf16[128,1024]{1,0:T(8,128)(2,1)S(1)} %get-tuple-element.41), channel_id=1, source_target_pairs={{0,2},{1,3},{2,0},{3,1},{4,6},{5,7},{6,4},{7,5},{8,10},{9,11},{10,... | collective-permute-start | bytes 786440 | tf_op jit(solution)/shard_map/ppermute | solution.py:236
  27.0 41.9 %collective-permute-start.2 = (bf16[128,1024]{1,0:T(8,128)(2,1)S(1)}, bf16[128,1024]{1,0:T(8,128)(2,1)S(1)}, u32[]{:S(2)}, u32[]{:S(2)}) collective-permute-start(bf16[128,1024]{1,0:T(8,128)(2,1)S(1)} %get-tuple-element.42), channel_id=1, source_target_pairs={{0,3},{1,2},{2,1},{3,0},{4,7},{5,6},{6,5},{7,4},{8,11},{9,10},{10,... | collective-permute-start | bytes 786440 | tf_op jit(solution)/shard_map/ppermute | solution.py:236
  27.5 25.7 %collective-permute-start.7 = (bf16[128,128]{1,0:T(8,128)(2,1)}, bf16[128,128]{1,0:T(8,128)(2,1)S(1)}, u32[]{:S(2)}, u32[]{:S(2)}) collective-permute-start(bf16[128,128]{1,0:T(8,128)(2,1)} %copy-done.12), channel_id=1, source_target_pairs={{0,2},{1,3},{2,0},{3,1},{4,6},{5,7},{6,4},{7,5},{8,10},{9,11},{10,... | collective-permute-start | bytes 98312 | tf_op jit(solution)/shard_map/ppermute | solution.py:236
  29.2 27.3 %collective-permute-start.8 = (bf16[128,128]{1,0:T(8,128)(2,1)}, bf16[128,128]{1,0:T(8,128)(2,1)S(1)}, u32[]{:S(2)}, u32[]{:S(2)}) collective-permute-start(bf16[128,128]{1,0:T(8,128)(2,1)} %copy-done.11), channel_id=1, source_target_pairs={{0,3},{1,2},{2,1},{3,0},{4,7},{5,6},{6,5},{7,4},{8,11},{9,10},{10,... | collective-permute-start | bytes 98312 | tf_op jit(solution)/shard_map/ppermute | solution.py:236
  53.3 5.9 %collective-permute-start.9 = (bf16[128,128]{1,0:T(8,128)(2,1)}, bf16[128,128]{1,0:T(8,128)(2,1)S(1)}, u32[]{:S(2)}, u32[]{:S(2)}) collective-permute-start(bf16[128,128]{1,0:T(8,128)(2,1)} %get-tuple-element.55), channel_id=1, source_target_pairs={{0,4},{1,5},{2,6},{3,7},{4,0},{5,1},{6,2},{7,3},{8,12},{9,13},{10,... | collective-permute-start | bytes 98312 | tf_op jit(solution)/shard_map/ppermute | solution.py:236
  56.5 4.2 %collective-permute-start.10 = (bf16[128,128]{1,0:T(8,128)(2,1)}, bf16[128,128]{1,0:T(8,128)(2,1)S(1)}, u32[]{:S(2)}, u32[]{:S(2)}) collective-permute-start(bf16[128,128]{1,0:T(8,128)(2,1)} %get-tuple-element.56), channel_id=1, source_target_pairs={{0,5},{1,4},{2,7},{3,6},{4,1},{5,0},{6,3},{7,2},{8,13},{9,12},{10,... | collective-permute-start | bytes 98312 | tf_op jit(solution)/shard_map/ppermute | solution.py:236
  59.1 5.0 %collective-permute-start.11 = (bf16[128,128]{1,0:T(8,128)(2,1)}, bf16[128,128]{1,0:T(8,128)(2,1)S(1)}, u32[]{:S(2)}, u32[]{:S(2)}) collective-permute-start(bf16[128,128]{1,0:T(8,128)(2,1)} %get-tuple-element.57), channel_id=1, source_target_pairs={{0,6},{1,7},{2,4},{3,5},{4,2},{5,3},{6,0},{7,1},{8,14},{9,15},{10,... | collective-permute-start | bytes 98312 | tf_op jit(solution)/shard_map/ppermute | solution.py:236
  60.7 15.2 %collective-permute-start.12 = (bf16[128,128]{1,0:T(8,128)(2,1)}, bf16[128,128]{1,0:T(8,128)(2,1)S(1)}, u32[]{:S(2)}, u32[]{:S(2)}) collective-permute-start(bf16[128,128]{1,0:T(8,128)(2,1)} %get-tuple-element.58), channel_id=1, source_target_pairs={{0,7},{1,6},{2,5},{3,4},{4,3},{5,2},{6,1},{7,0},{8,15},{9,14},{10,... | collective-permute-start | bytes 98312 | tf_op jit(solution)/shard_map/ppermute | solution.py:236
  64.2 12.5 %collective-permute-start.13 = (bf16[128,128]{1,0:T(8,128)(2,1)}, bf16[128,128]{1,0:T(8,128)(2,1)S(1)}, u32[]{:S(2)}, u32[]{:S(2)}) collective-permute-start(bf16[128,128]{1,0:T(8,128)(2,1)} %copy-done.10), channel_id=1, source_target_pairs={{0,8},{1,9},{2,10},{3,11},{4,12},{5,13},{6,14},{7,15},{8,0},{9,1},... | collective-permute-start | bytes 98312 | tf_op jit(solution)/shard_map/ppermute | solution.py:236
  68.2 12.6 %collective-permute-start.14 = (bf16[128,128]{1,0:T(8,128)(2,1)}, bf16[128,128]{1,0:T(8,128)(2,1)S(1)}, u32[]{:S(2)}, u32[]{:S(2)}) collective-permute-start(bf16[128,128]{1,0:T(8,128)(2,1)} %copy-done.9), channel_id=1, source_target_pairs={{0,9},{1,8},{2,11},{3,10},{4,13},{5,12},{6,15},{7,14},{8,1},{9,0},... | collective-permute-start | bytes 98312 | tf_op jit(solution)/shard_map/ppermute | solution.py:236
  68.2 12.7 %collective-permute-start.15 = (bf16[128,128]{1,0:T(8,128)(2,1)}, bf16[128,128]{1,0:T(8,128)(2,1)S(1)}, u32[]{:S(2)}, u32[]{:S(2)}) collective-permute-start(bf16[128,128]{1,0:T(8,128)(2,1)} %copy-done.8), channel_id=1, source_target_pairs={{0,10},{1,11},{2,8},{3,9},{4,14},{5,15},{6,12},{7,13},{8,2},{9,3},... | collective-permute-start | bytes 98312 | tf_op jit(solution)/shard_map/ppermute | solution.py:236
  68.8 14.3 %collective-permute-start.16 = (bf16[128,128]{1,0:T(8,128)(2,1)}, bf16[128,128]{1,0:T(8,128)(2,1)S(1)}, u32[]{:S(2)}, u32[]{:S(2)}) collective-permute-start(bf16[128,128]{1,0:T(8,128)(2,1)} %copy-done.7), channel_id=1, source_target_pairs={{0,11},{1,10},{2,9},{3,8},{4,15},{5,14},{6,13},{7,12},{8,3},{9,2},... | collective-permute-start | bytes 98312 | tf_op jit(solution)/shard_map/ppermute | solution.py:236
  75.8 17.5 %collective-permute-start.3 = (bf16[128,256]{1,0:T(8,128)(2,1)S(1)}, bf16[128,256]{1,0:T(8,128)(2,1)S(1)}, u32[]{:S(2)}, u32[]{:S(2)}) collective-permute-start(bf16[128,256]{1,0:T(8,128)(2,1)S(1)} %get-tuple-element.45), channel_id=1, source_target_pairs={{0,1},{1,0},{2,3},{3,2},{4,5},{5,4},{6,7},{7,6},{8,9},{9,8},{10,11... | collective-permute-start | bytes 196616 | tf_op jit(solution)/shard_map/ppermute | solution.py:236
  76.7 11.9 %collective-permute-start.17 = (bf16[128,128]{1,0:T(8,128)(2,1)}, bf16[128,128]{1,0:T(8,128)(2,1)S(1)}, u32[]{:S(2)}, u32[]{:S(2)}) collective-permute-start(bf16[128,128]{1,0:T(8,128)(2,1)} %copy-done.6), channel_id=1, source_target_pairs={{0,12},{1,13},{2,14},{3,15},{4,8},{5,9},{6,10},{7,11},{8,4},{9,5},... | collective-permute-start | bytes 98312 | tf_op jit(solution)/shard_map/ppermute | solution.py:236
  80.7 8.7 %collective-permute-start.18 = (bf16[128,128]{1,0:T(8,128)(2,1)}, bf16[128,128]{1,0:T(8,128)(2,1)S(1)}, u32[]{:S(2)}, u32[]{:S(2)}) collective-permute-start(bf16[128,128]{1,0:T(8,128)(2,1)} %copy-done.5), channel_id=1, source_target_pairs={{0,13},{1,12},{2,15},{3,14},{4,9},{5,8},{6,11},{7,10},{8,5},{9,4},... | collective-permute-start | bytes 98312 | tf_op jit(solution)/shard_map/ppermute | solution.py:236
  80.8 9.8 %collective-permute-start.19 = (bf16[128,128]{1,0:T(8,128)(2,1)S(1)}, bf16[128,128]{1,0:T(8,128)(2,1)S(1)}, u32[]{:S(2)}, u32[]{:S(2)}) collective-permute-start(bf16[128,128]{1,0:T(8,128)(2,1)S(1)} %get-tuple-element.65), channel_id=1, source_target_pairs={{0,14},{1,15},{2,12},{3,13},{4,10},{5,11},{6,8},{7,9},{8,6},{9,7},... | collective-permute-start | bytes 98312 | tf_op jit(solution)/shard_map/ppermute | solution.py:236
  83.1 7.6 %collective-permute-start.20 = (bf16[128,128]{1,0:T(8,128)(2,1)S(1)}, bf16[128,128]{1,0:T(8,128)(2,1)S(1)}, u32[]{:S(2)}, u32[]{:S(2)}) collective-permute-start(bf16[128,128]{1,0:T(8,128)(2,1)S(1)} %get-tuple-element.66), channel_id=1, source_target_pairs={{0,15},{1,14},{2,13},{3,12},{4,11},{5,10},{6,9},{7,8},{8,7},{9,6},... | collective-permute-start | bytes 98312 | tf_op jit(solution)/shard_map/ppermute | solution.py:236
  88.5 5.3 %collective-permute-start.4 = (bf16[128,256]{1,0:T(8,128)(2,1)S(1)}, bf16[128,256]{1,0:T(8,128)(2,1)S(1)}, u32[]{:S(2)}, u32[]{:S(2)}) collective-permute-start(bf16[128,256]{1,0:T(8,128)(2,1)S(1)} %get-tuple-element.46), channel_id=1, source_target_pairs={{0,2},{1,3},{2,0},{3,1},{4,6},{5,7},{6,4},{7,5},{8,10},{9,11},{10,... | collective-permute-start | bytes 196616 | tf_op jit(solution)/shard_map/ppermute | solution.py:236
  89.4 5.0 %collective-permute-start.5 = (bf16[128,256]{1,0:T(8,128)(2,1)S(1)}, bf16[128,256]{1,0:T(8,128)(2,1)S(1)}, u32[]{:S(2)}, u32[]{:S(2)}) collective-permute-start(bf16[128,256]{1,0:T(8,128)(2,1)S(1)} %get-tuple-element.47), channel_id=1, source_target_pairs={{0,3},{1,2},{2,1},{3,0},{4,7},{5,6},{6,5},{7,4},{8,11},{9,10},{10,... | collective-permute-start | bytes 196616 | tf_op jit(solution)/shard_map/ppermute | solution.py:236
  91.9 2.5 %collective-permute-start.21 = (bf16[128,256]{1,0:T(8,128)(2,1)S(1)}, bf16[128,256]{1,0:T(8,128)(2,1)S(1)}, u32[]{:S(2)}, u32[]{:S(2)}) collective-permute-start(bf16[128,256]{1,0:T(8,128)(2,1)S(1)} %get-tuple-element.68), channel_id=1, source_target_pairs={{0,1},{1,0},{2,3},{3,2},{4,5},{5,4},{6,7},{7,6},{8,9},{9,8},{10,11... | collective-permute-start | bytes 196616 | tf_op jit(solution)/shard_map/ppermute | solution.py:236
  92.1 4.5 %collective-permute-start.22 = (bf16[128,256]{1,0:T(8,128)(2,1)S(1)}, bf16[128,256]{1,0:T(8,128)(2,1)S(1)}, u32[]{:S(2)}, u32[]{:S(2)}) collective-permute-start(bf16[128,256]{1,0:T(8,128)(2,1)S(1)} %get-tuple-element.69), channel_id=1, source_target_pairs={{0,2},{1,3},{2,0},{3,1},{4,6},{5,7},{6,4},{7,5},{8,10},{9,11},{10,... | collective-permute-start | bytes 196616 | tf_op jit(solution)/shard_map/ppermute | solution.py:236
  93.4 4.4 %collective-permute-start.23 = (bf16[128,256]{1,0:T(8,128)(2,1)S(1)}, bf16[128,256]{1,0:T(8,128)(2,1)S(1)}, u32[]{:S(2)}, u32[]{:S(2)}) collective-permute-start(bf16[128,256]{1,0:T(8,128)(2,1)S(1)} %get-tuple-element.70), channel_id=1, source_target_pairs={{0,3},{1,2},{2,1},{3,0},{4,7},{5,6},{6,5},{7,4},{8,11},{9,10},{10,... | collective-permute-start | bytes 196616 | tf_op jit(solution)/shard_map/ppermute | solution.py:236
  (15 other events, 42.5 us)

commit v2 on v1

--- a/solution.py
+++ b/solution.py
@@ -5,11 +5,14 @@
 from jax.experimental.pallas import tpu as pltpu
 from jax.sharding import PartitionSpec as P
 
+
 HEADS = 16
 KV_HEADS = 8
 HEAD_DIM = 128
 DEPTHS = 4
 MEMBERS = 4
+STAGE_VMEM = 60 * 1024 * 2**10
+PIECES_VMEM = 52 * 2**20
 GROUP = HEADS // KV_HEADS
 
 query_scale = 168.0 ** (-0.5)
@@ -24,53 +27,57 @@
     return lax.dot_general(a, b, (((1,), (0,)), ((), ())), preferred_element_type=jnp.float32)
 
 
-def stage_kernel(parent, up, owner, slot, queries, seg_kv, store, *rest):
-    send, p0, p1, p2, p3, bias = rest[:6]
-    late, (picks, sems) = rest[6:-2], rest[-2:]
+def walk(parent, up, g):
+    out = [parent[g]]
+    for _ in range(DEPTHS - 1):
+        out.append(jnp.where(out[-1] >= 0, up[jnp.maximum(out[-1], 0)], -1))
+    return out
+
+
+def stage_kernel(parent_in, up_in, owner_in, slot_in, store, send, picks, parent, up, owner, slot, sems):
+    tables = ((parent_in, parent), (up_in, up), (owner_in, owner), (slot_in, slot))
+    copies = [pltpu.make_async_copy(src, dst, sems.at[i]) for i, (src, dst) in enumerate(tables)]
+    for c in copies:
+        c.start()
     me = lax.axis_index("nodes")
-    member = me % MEMBERS
-    segment = me // MEMBERS
     segs = parent.shape[0]
-    blocks, pages = owner.shape
-    q_cols = queries.shape[1] // MEMBERS
-    kv_cols = seg_kv.shape[2] // MEMBERS
-
-    def path_rows(g):
-        rows = lax.broadcasted_iota(jnp.int32, (blocks, 1), 0)
-        current = parent[g]
-        on_path = rows == current
-        for _ in range(DEPTHS - 1):
-            current = jnp.where(current >= 0, up[jnp.maximum(current, 0)], -1)
-            on_path = on_path | (rows == current)
-        return on_path
-
-    held = owner[...] == me
-    pick_of = jnp.max(jnp.where(held, slot[...], 0), axis=1, keepdims=True)
+    _, blocks = owner.shape
+    kv_cols = store.shape[3] // MEMBERS
+    sem = sems.at[len(copies)]
+    for c in copies:
+        c.wait()
+    pick_of = jnp.max(jnp.where(owner[...] == me, slot[...], 0), axis=0, keepdims=True)
+    lanes = lax.broadcasted_iota(jnp.int32, (1, blocks), 1)
 
     def one_segment(g, carry):
-        pick = jnp.max(jnp.where(path_rows(g), pick_of, 0))
+        on_path = lanes < 0
+        for block in walk(parent, up, g):
+            on_path = on_path | (lanes == block)
+        pick = jnp.max(jnp.where(on_path, pick_of, 0))
         picks[g] = pick
         for m in range(MEMBERS):
             to = g * MEMBERS + m
             col = m * kv_cols
-            pltpu.make_async_copy(
-                store.at[0, pick, :, pl.ds(col, HEAD_DIM)], send.at[to, 0], sems.at[4]
-            ).start()
-            pltpu.make_async_copy(
-                store.at[0, pick, :, pl.ds(col + HEAD_DIM, HEAD_DIM)], send.at[to, 1], sems.at[4]
-            ).start()
-            pltpu.make_async_copy(
-                store.at[1, pick, :, pl.ds(col, HEAD_DIM)], send.at[to, 2], sems.at[4]
-            ).start()
+            for i, (kind, at) in enumerate(((0, col), (0, col + HEAD_DIM), (1, col))):
+                pltpu.make_async_copy(store.at[kind, pick, :, pl.ds(at, HEAD_DIM)], send.at[to, i], sem).start()
         return carry
 
     lax.fori_loop(0, segs, one_segment, 0, unroll=segs <= 4)
-    for d, ref in enumerate(late):
-        to = me ^ d
-        col = pl.multiple_of(to % MEMBERS * kv_cols, kv_cols) + HEAD_DIM
-        pltpu.make_async_copy(
-            store.at[1, picks[to // MEMBERS], :, pl.ds(pl.multiple_of(col, HEAD_DIM), HEAD_DIM)], ref, sems.at[5 + d]
-        ).start()
+    pltpu.make_async_copy(send, send, sem).wait()
+
+
+def late_place(g, tok, page_tok):
+    stack = tok // page_tok
+    return g % stack * page_tok, g // stack
+
+
+def pieces_kernel(parent, up, owner, picks, queries, seg_kv, store, p0, p1, p2, p3, bias, sems):
+    member = lax.axis_index("nodes") % MEMBERS
+    tok = queries.shape[0]
+    page_tok = store.shape[2]
+    q_cols = queries.shape[1] // MEMBERS
+    kv_cols = seg_kv.shape[2] // MEMBERS
+    own_cols = q_cols + 2 * kv_cols
     for d, piece in enumerate((p0, p1, p2, p3)):
         to = member ^ d
         q_at = pl.multiple_of(to * q_cols, q_cols)
@@ -82,17 +89,58 @@
                 piece.at[:, pl.ds(q_cols + i * kv_cols, kv_cols)],
                 sems.at[d],
             ).start()
-    page_tok = store.shape[2]
-    mine = path_rows(segment)
-    for at in range(0, bias.shape[1], 128):
-        page = (lax.broadcasted_iota(jnp.int32, (blocks, 128), 1) + at) // page_tok
-        found = jnp.zeros((blocks, 128), jnp.float32)
+        col = pl.multiple_of(to * kv_cols + HEAD_DIM, HEAD_DIM)
+        for g in range(parent.shape[0]):
+            row, block = late_place(g, tok, page_tok)
+            pltpu.make_async_copy(
+                store.at[1, picks[g], :, pl.ds(col, HEAD_DIM)],
+                piece.at[pl.ds(row, page_tok), pl.ds(own_cols + block * HEAD_DIM, HEAD_DIM)],
+                sems.at[d],
+            ).start()
+    page_bias(parent, up, owner, bias, page_tok)
+    for i, ref in enumerate((p0, p1, p2, p3)):
+        pltpu.make_async_copy(ref, ref, sems.at[i]).wait()
+
+
+def relay_kernel(p0, p1, p2, p3, *rest):
+    outs, sems = rest[:-1], rest[-1]
+    me = lax.axis_index("nodes")
+    member, segment = me % MEMBERS, me // MEMBERS
+    tok, cols = p0.shape
+    page_tok = outs[0].shape[1]
+    late_cols = len(outs) * page_tok * HEAD_DIM // tok
+    for e, out in enumerate(outs):
+        row, block = late_place(segment ^ e, tok, page_tok)
+        col = pl.multiple_of(cols - late_cols + block * HEAD_DIM, HEAD_DIM)
+        row = pl.multiple_of(row, page_tok)
+        for d, piece in enumerate((p0, p1, p2, p3)):
+            pltpu.make_async_copy(
+                piece.at[pl.ds(row, page_tok), pl.ds(col, HEAD_DIM)], out.at[member ^ d], sems.at[e]
+            ).start()
+    for e, out in enumerate(outs):
+        pltpu.make_async_copy(out, out, sems.at[e]).wait()
+
+
+def page_bias(parent, up, owner, bias_ref, page_tok):
+    pages, blocks = owner.shape
+    path = walk(parent, up, lax.axis_index("nodes") // MEMBERS)
+    rows = lax.broadcasted_iota(jnp.int32, (8, blocks), 0)
+    block_at = jnp.full((8, blocks), -1, jnp.int32)
+    for i, block in enumerate(path):
+        block_at = jnp.where(rows == i, block, block_at)
+    chosen = (lax.broadcasted_iota(jnp.int32, (8, blocks), 1) == block_at).astype(jnp.float32)
+    above = owner[...].astype(jnp.float32) + 1.0
+    held_by = lax.dot_general(
+        chosen, above, (((1,), (1,)), ((), ())), precision=lax.Precision.HIGHEST, preferred_element_type=jnp.float32
+    )
+    held_by = (held_by + 0.5).astype(jnp.int32) - 1
+    for at in range(0, bias_ref.shape[1], 128):
+        page = (lax.broadcasted_iota(jnp.int32, (8, 128), 1) + at) // page_tok
+        found = jnp.zeros((8, 128), jnp.float32)
         for p in range(pages):
-            found = jnp.where(mine & (owner[:, p : p + 1] == page), 1.0, found)
+            found = jnp.where(held_by[:, p : p + 1] == page, 1.0, found)
         found = jnp.max(found, axis=0, keepdims=True)
-        bias[:, at : at + 128] = jnp.where(found > 0.0, 0.0, -jnp.inf)
-    for i, ref in enumerate((p0, p1, p2, p3, send, *late)):
-        pltpu.make_async_copy(ref, ref, sems.at[i]).wait()
+        bias_ref[:, at : at + 128] = jnp.where(found > 0.0, 0.0, -jnp.inf)
 
 
 def head_inputs(pieces, h, q_cols, kv_cols):
@@ -132,7 +180,7 @@
 def full_kernel(page_tok, h, bias_ref, p0, p1, p2, p3, pages, o0, o1, o2, o3, score_ref):
     member = lax.axis_index("nodes") % MEMBERS
     tok = p0.shape[0]
-    q_cols = p0.shape[1] // 2
+    q_cols = HEADS // MEMBERS * HEAD_DIM
     kv_cols = q_cols // GROUP
     queries, k_own, v_own = head_inputs((p0, p1, p2, p3), h, q_cols, kv_cols)
     keys = pages.shape[0] * page_tok
@@ -156,7 +204,7 @@
 def weights_kernel(page_tok, h, bias_ref, p0, p1, p2, p3, pages, w_ref, mixed_ref, total_ref, score_ref):
     member = lax.axis_index("nodes") % MEMBERS
     tok = p0.shape[0]
-    q_cols = p0.shape[1] // 2
+    q_cols = HEADS // MEMBERS * HEAD_DIM
     kv_cols = q_cols // GROUP
     queries, k_own, v_own = head_inputs((p0, p1, p2, p3), h, q_cols, kv_cols)
     keys = pages.shape[0] * page_tok
@@ -178,9 +226,10 @@
     late, outs, v_ref = rest[: -MEMBERS - 1], rest[-MEMBERS - 1 : -1], rest[-1]
     me = lax.axis_index("nodes")
     tok = outs[0].shape[0]
-    page_tok = late[0].shape[0]
-    for d, ref in enumerate(late):
-        v_ref[pl.ds(pl.multiple_of((me ^ d) * page_tok, page_tok), page_tok)] = ref[...]
+    rows = MEMBERS * late[0].shape[1]
+    for e, ref in enumerate(late):
+        at = pl.multiple_of((me // MEMBERS ^ e) * rows, rows)
+        v_ref[pl.ds(at, rows)] = ref[...].reshape(rows, HEAD_DIM)
     for d, out in enumerate(outs):
         mixed = mixed_ref[d] + dot(w_ref[d], v_ref[...])
         res = (mixed / total_ref[d]).astype(jnp.bfloat16)
@@ -206,38 +255,62 @@
 
 def local(queries, seg_kv, kv_store, seg_parent, block_up, page_owner, page_slot):
     nodes = lax.axis_size("nodes")
+    segs = nodes // MEMBERS
     tok = queries.shape[0]
     page_tok = kv_store.shape[2]
     keys = nodes * page_tok
-    bf16, f32 = jnp.bfloat16, jnp.float32
-    any_spec = pl.BlockSpec(memory_space=pl.ANY)
+    bf16, f32, i32 = jnp.bfloat16, jnp.float32, jnp.int32
+    hbm = pl.BlockSpec(memory_space=pltpu.HBM)
     smem = pl.BlockSpec(memory_space=pltpu.SMEM)
     vmem = pl.BlockSpec(memory_space=pltpu.VMEM)
     params = pltpu.CompilerParams(vmem_limit_bytes=24 * 2**20)
-    piece = jax.ShapeDtypeStruct((tok, queries.shape[1] // MEMBERS + 2 * seg_kv.shape[2] // MEMBERS), bf16)
-    late = jax.ShapeDtypeStruct((page_tok, HEAD_DIM), bf16)
+    wide = pltpu.CompilerParams(vmem_limit_bytes=STAGE_VMEM)
+    late_cols = segs * page_tok * HEAD_DIM // tok
+    piece_cols = (queries.shape[1] + 2 * seg_kv.shape[2]) // MEMBERS + late_cols
+    piece = jax.ShapeDtypeStruct((tok, piece_cols), bf16)
+    late = jax.ShapeDtypeStruct((MEMBERS, page_tok, HEAD_DIM), bf16)
     early = jax.ShapeDtypeStruct((nodes, 3, page_tok, HEAD_DIM), bf16)
-    staged = pl.pallas_call(
+    owner_of, slot_of = page_owner.T, page_slot.T
+    send, picks = pl.pallas_call(
         stage_kernel,
-        in_specs=[smem] * 2 + [vmem] * 2 + [any_spec] * 3,
-        out_specs=[vmem] * (6 + nodes),
-        out_shape=[early, *[piece] * MEMBERS, jax.ShapeDtypeStruct((1, keys), f32), *[late] * nodes],
-        scratch_shapes=[pltpu.SMEM((nodes // MEMBERS,), jnp.int32), pltpu.SemaphoreType.DMA((5 + nodes,))],
-        compiler_params=params,
+        in_specs=[hbm] * 5,
+        out_specs=[vmem, smem],
+        out_shape=[early, jax.ShapeDtypeStruct((segs,), i32)],
+        scratch_shapes=[
+            pltpu.SMEM(seg_parent.shape, i32),
+            pltpu.SMEM(block_up.shape, i32),
+            pltpu.VMEM(owner_of.shape, i32),
+            pltpu.VMEM(slot_of.shape, i32),
+            pltpu.SemaphoreType.DMA((5,)),
+        ],
+        compiler_params=wide,
         name="stage",
-    )(seg_parent, block_up, page_owner, page_slot, queries, seg_kv, kv_store)
-    send, p0, p1, p2, p3, bias = staged[:6]
-    held = staged[6:]
-
-    def exchange(x):
-        return lax.all_to_all(x, "nodes", split_axis=0, concat_axis=0, tiled=True)
+    )(seg_parent, block_up, owner_of, slot_of, kv_store)
+    *sends, bias = pl.pallas_call(
+        pieces_kernel,
+        in_specs=[smem] * 2 + [vmem] + [smem] + [hbm] * 3,
+        out_specs=[vmem] * (MEMBERS + 1),
+        out_shape=[piece] * MEMBERS + [jax.ShapeDtypeStruct((1, keys), f32)],
+        scratch_shapes=[pltpu.SemaphoreType.DMA((MEMBERS,))],
+        compiler_params=pltpu.CompilerParams(vmem_limit_bytes=PIECES_VMEM),
+        name="pieces",
+    )(seg_parent, block_up, owner_of, picks, queries, seg_kv, kv_store)
 
     def swapped(x, d):
         return lax.ppermute(x, "nodes", [(i, i ^ d) for i in range(nodes)])
 
-    got = exchange(send)
-    pieces = (p0, swapped(p1, 1), swapped(p2, 2), swapped(p3, 3))
-    values = [held[0]] + [swapped(held[d], d) for d in range(1, nodes)]
+    got = lax.all_to_all(send, "nodes", split_axis=0, concat_axis=0, tiled=True)
+    pieces = [sends[0]] + [swapped(sends[d], d) for d in range(1, MEMBERS)]
+    held = pl.pallas_call(
+        relay_kernel,
+        in_specs=[vmem] * MEMBERS,
+        out_specs=[vmem] * segs,
+        out_shape=[late] * segs,
+        scratch_shapes=[pltpu.SemaphoreType.DMA((segs,))],
+        compiler_params=params,
+        name="relay",
+    )(*pieces)
+    values = [held[0]] + [swapped(held[e], e * MEMBERS) for e in range(1, segs)]
     rows = GROUP * tok
     scratch = [pltpu.VMEM((rows, keys), f32)]
     out_piece = jax.ShapeDtypeStruct((tok, GROUP * HEAD_DIM), bf16)
@@ -265,7 +338,7 @@
     )(bias, *pieces, got)
     out_b = pl.pallas_call(
         values_kernel,
-        in_specs=[vmem] * (3 + nodes),
+        in_specs=[vmem] * (3 + segs),
         out_specs=[vmem] * 4,
         out_shape=[out_piece] * 4,
         scratch_shapes=[pltpu.VMEM((keys, HEAD_DIM), bf16)],
@@ -278,7 +351,7 @@
     return pl.pallas_call(
         join_kernel,
         in_specs=[vmem] * 8,
-        out_specs=any_spec,
+        out_specs=hbm,
         out_shape=jax.ShapeDtypeStruct(queries.shape, bf16),
         scratch_shapes=[pltpu.SemaphoreType.DMA((8,))],
         compiler_params=params,

time: 99 us -> 71.9 us (0.73)
  the two profiles are of different devices: /device:TPU:0 before, /device:TPU:16 now
where the time goes in v2:
time: 71.9 us; the launch traced here: 70.6 us
  waiting for transfers between devices  36.1 us (50%)
  Pallas kernels  17.3 us (24%)
  starting transfers between devices  16.4 us (23%)
    ppermute x12, waiting for transfers between devices, swapped(): return lax.ppermute(x, 'nodes', [(i, i ^ d) for i in range(nodes)])  36.1 us
    ppermute x12, starting transfers between devices, swapped(): return lax.ppermute(x, 'nodes', [(i, i ^ d) for i in range(nodes)])  10.2 us
    all_to_all x1, starting transfers between devices, local(): got = lax.all_to_all(send, 'nodes', split_axis=0, concat_axis=0, tiled=True)  6.17 us
    pallas_call x1, Pallas kernels, local(): pl.pallas_call(lambda *refs: full_kernel(page_tok, 0, *refs), in_specs=[v...  4.29 us
    pallas_call x1, Pallas kernels, local(): pl.pallas_call(stage_kernel, in_specs=[hbm] * 5, out_specs=[vmem, smem],...  3.59 us
    pallas_call x1, Pallas kernels, local(): pl.pallas_call(lambda *refs: weights_kernel(page_tok, 1, *refs), in_specs...  3.44 us
    pallas_call x1, Pallas kernels, local(): pl.pallas_call(values_kernel, in_specs=[vmem] * (3 + segs), out_specs=[vm...  2.19 us
    pallas_call x1, Pallas kernels, local(): pl.pallas_call(pieces_kernel, in_specs=[smem] * 2 + [vmem] + [smem] + [hb...  2.01 us
  transfers between devices with their start and end apart: 13, of which 5 were waited for; matrix products, arithmetic and copies ran while one was open for 0% of the time, Pallas kernels for 18%

profile of v2, /device:TPU:16, one launch (start us, length us, event | category | flops | bytes accessed | tf_op | source)
XLA Modules:
  0.0 70.6 jit_solution(5342959969816606733)
XLA Ops:
  0.0 3.6 %stage.1 = (bf16[16,3,128,128]{3,2,1,0:T(8,128)(2,1)}, s32[4]{0:T(128)}) custom-call(s32[4]{0:T(128)} %parent.1, s32[40]{0:T(128)} %up.1, s32[4,40]{1,0:T(4,128)} %bitcast.2, s32[4,40]{1,0:T(4,128)} %bitcast.4, bf16[2,27,128,1024]{3,2,1,0:T(8,128)(2,1)} %store.3), custom_call_target="tpu_custom_call" | custom-call | tf_op jit(solution)/shard_map/stage/pallas_call | solution.py:274
  3.6 6.2 %all-to-all-start = ((bf16[16,3,128,128]{3,2,1,0:T(8,128)(2,1)}), bf16[16,3,128,128]{3,2,1,0:T(8,128)(2,1)S(1)}, u32[]{:S(2)}, u32[]{:S(2)}) async-start(bf16[16,3,128,128]{3,2,1,0:T(8,128)(2,1)} %get-tuple-element.33), calls=%async_computation | async-start | bytes 3145728 | tf_op jit(solution)/shard_map/all_to_all | solution.py:302
  9.8 0.6 copy-done.3
  10.5 2.0 %pieces.1 = (bf16[128,1536]{1,0:T(8,128)(2,1)S(1)}, bf16[128,1536]{1,0:T(8,128)(2,1)S(1)}, bf16[128,1536]{1,0:T(8,128)(2,1)S(1)}, bf16[128,1536]{1,0:T(8,128)(2,1)S(1)}, f32[1,2048]{1,0:T(1,128)S(1)}) custom-call(s32[4]{0:T(128)S(1)} %copy-done.1, s32[40]{0:T(128)S(1)} %copy-done.2, s32[4,40]{1,0:T(4,128)S(1)} %bitcast.3, s32[4]{0:T(128)S(1)} %copy-done.3, ...), custom_call_target="tpu_custom_call" | custom-call | tf_op jit(solution)/shard_map/pieces/pallas_call | solution.py:289
  12.5 0.2 collective-permute-start
  12.7 1.5 %collective-permute-start.1 = (bf16[128,1536]{1,0:T(8,128)(2,1)S(1)}, bf16[128,1536]{1,0:T(8,128)(2,1)S(1)}, u32[]{:S(2)}, u32[]{:S(2)}) collective-permute-start(bf16[128,1536]{1,0:T(8,128)(2,1)S(1)} %get-tuple-element.31), channel_id=1, source_target_pairs={{0,2},{1,3},{2,0},{3,1},{4,6},{5,7},{6,4},{7,5},{8,10},{9,11},{10,... | collective-permute-start | bytes 1179656 | tf_op jit(solution)/shard_map/ppermute | solution.py:300
  14.1 0.3 collective-permute-start.2
  14.4 18.2 %collective-permute-done.1.refs_3_.p2 = bf16[128,1536]{1,0:T(8,128)(2,1)S(1)} collective-permute-done((bf16[128,1536]{1,0:T(8,128)(2,1)S(1)}, bf16[128,1536]{1,0:T(8,128)(2,1)S(1)}, u32[]{:S(2)}, u32[]{:S(2)}) %collective-permute-start.1) | collective-permute-done | bytes 393248 | tf_op jit(solution)/shard_map/ppermute | solution.py:300
  32.6 11.6 %collective-permute-done.2.refs_4_.p3 = bf16[128,1536]{1,0:T(8,128)(2,1)S(1)} collective-permute-done((bf16[128,1536]{1,0:T(8,128)(2,1)S(1)}, bf16[128,1536]{1,0:T(8,128)(2,1)S(1)}, u32[]{:S(2)}, u32[]{:S(2)}) %collective-permute-start.2) | collective-permute-done | bytes 393248 | tf_op jit(solution)/shard_map/ppermute | solution.py:300
  44.2 0.9 %relay.1 = (bf16[4,128,128]{2,1,0:T(8,128)(2,1)S(1)}, bf16[4,128,128]{2,1,0:T(8,128)(2,1)}, bf16[4,128,128]{2,1,0:T(8,128)(2,1)}, bf16[4,128,128]{2,1,0:T(8,128)(2,1)}) custom-call(bf16[128,1536]{1,0:T(8,128)(2,1)S(1)} %get-tuple-element.29.refs_1_.p0, bf16[128,1536]{1,0:T(8,128)(2,1)S(1)} %collective-permute-done.refs_2_.p1, ...), custom_call_target="tpu_custom_call" | custom-call | tf_op jit(solution)/shard_map/relay/pallas_call | solution.py:304
  45.1 2.9 %collective-permute-start.6 = (bf16[4,128,128]{2,1,0:T(8,128)(2,1)}, bf16[4,128,128]{2,1,0:T(8,128)(2,1)S(1)}, u32[]{:S(2)}, u32[]{:S(2)}) collective-permute-start(bf16[4,128,128]{2,1,0:T(8,128)(2,1)} %get-tuple-element.42), channel_id=1, source_target_pairs={{0,4},{1,5},{2,6},{3,7},{4,0},{5,1},{6,2},{7,3},{8,12},{9,13},{10,... | collective-permute-start | bytes 393224 | tf_op jit(solution)/shard_map/ppermute | solution.py:300
  48.0 0.4 collective-permute-start.7
  48.4 1.1 %collective-permute-start.8 = (bf16[4,128,128]{2,1,0:T(8,128)(2,1)}, bf16[4,128,128]{2,1,0:T(8,128)(2,1)}, u32[]{:S(2)}, u32[]{:S(2)}) collective-permute-start(bf16[4,128,128]{2,1,0:T(8,128)(2,1)} %get-tuple-element.44), channel_id=1, source_target_pairs={{0,12},{1,13},{2,14},{3,15},{4,8},{5,9},{6,10},{7,11},{8,4},{9,5},... | collective-permute-start | bytes 393224 | tf_op jit(solution)/shard_map/ppermute | solution.py:300
  49.5 4.3 %full.1 = (bf16[128,256]{1,0:T(8,128)(2,1)S(1)}, bf16[128,256]{1,0:T(8,128)(2,1)S(1)}, bf16[128,256]{1,0:T(8,128)(2,1)S(1)}, bf16[128,256]{1,0:T(8,128)(2,1)S(1)}) custom-call(f32[1,2048]{1,0:T(1,128)S(1)} %get-tuple-element.28.refs_0_, bf16[128,1536]{1,0:T(8,128)(2,1)S(1)} %get-tuple-element.29.refs_1_.p0, ...), custom_call_target="tpu_custom_call" | custom-call | tf_op jit(solution)/shard_map/full/pallas_call | solution.py:317
  53.9 1.1 %collective-permute-start.4 = (bf16[128,256]{1,0:T(8,128)(2,1)S(1)}, bf16[128,256]{1,0:T(8,128)(2,1)S(1)}, u32[]{:S(2)}, u32[]{:S(2)}) collective-permute-start(bf16[128,256]{1,0:T(8,128)(2,1)S(1)} %get-tuple-element.36), channel_id=1, source_target_pairs={{0,2},{1,3},{2,0},{3,1},{4,6},{5,7},{6,4},{7,5},{8,10},{9,11},{10,... | collective-permute-start | bytes 196616 | tf_op jit(solution)/shard_map/ppermute | solution.py:300
  55.0 3.4 %weights.1 = (bf16[4,256,2048]{2,1,0:T(8,128)(2,1)S(1)}, f32[4,256,128]{2,1,0:T(8,128)S(1)}, f32[4,256,128]{2,1,0:T(8,128)S(1)}) custom-call(f32[1,2048]{1,0:T(1,128)S(1)} %get-tuple-element.28.refs_0_, bf16[128,1536]{1,0:T(8,128)(2,1)S(1)} %get-tuple-element.29.refs_1_.p0, bf16[128,1536]{1,0:T(8,128)(2,1)S(1)} %collective-permute-done.refs_2_.p1, ...), custom_call_target="tpu_custom_call" | custom-call | tf_op jit(solution)/shard_map/weights/pallas_call | solution.py:326
  58.4 0.8 %collective-permute-start.5 = (bf16[128,256]{1,0:T(8,128)(2,1)S(1)}, bf16[128,256]{1,0:T(8,128)(2,1)S(1)}, u32[]{:S(2)}, u32[]{:S(2)}) collective-permute-start(bf16[128,256]{1,0:T(8,128)(2,1)S(1)} %get-tuple-element.37), channel_id=1, source_target_pairs={{0,3},{1,2},{2,1},{3,0},{4,7},{5,6},{6,5},{7,4},{8,11},{9,10},{10,... | collective-permute-start | bytes 196616 | tf_op jit(solution)/shard_map/ppermute | solution.py:300
  59.3 2.8 %collective-permute-done.8.rest_3_ = bf16[4,128,128]{2,1,0:T(8,128)(2,1)} collective-permute-done((bf16[4,128,128]{2,1,0:T(8,128)(2,1)}, bf16[4,128,128]{2,1,0:T(8,128)(2,1)}, u32[]{:S(2)}, u32[]{:S(2)}) %collective-permute-start.8) | collective-permute-done | bytes 131104 | tf_op jit(solution)/shard_map/ppermute | solution.py:300
  62.1 2.2 %values.1 = (bf16[128,256]{1,0:T(8,128)(2,1)S(1)}, bf16[128,256]{1,0:T(8,128)(2,1)S(1)}, bf16[128,256]{1,0:T(8,128)(2,1)S(1)}, bf16[128,256]{1,0:T(8,128)(2,1)S(1)}) custom-call(bf16[4,256,2048]{2,1,0:T(8,128)(2,1)S(1)} %get-tuple-element.38.w_ref, f32[4,256,128]{2,1,0:T(8,128)S(1)} %get-tuple-element.39.mixed_ref, ...), custom_call_target="tpu_custom_call" | custom-call | tf_op jit(solution)/shard_map/values/pallas_call | solution.py:339
  64.4 0.7 collective-permute-start.10
  65.0 1.2 %collective-permute-start.11 = (bf16[128,256]{1,0:T(8,128)(2,1)S(1)}, bf16[128,256]{1,0:T(8,128)(2,1)S(1)}, u32[]{:S(2)}, u32[]{:S(2)}) collective-permute-start(bf16[128,256]{1,0:T(8,128)(2,1)S(1)} %get-tuple-element.48), channel_id=1, source_target_pairs={{0,3},{1,2},{2,1},{3,0},{4,7},{5,6},{6,5},{7,4},{8,11},{9,10},{10,... | collective-permute-start | bytes 196616 | tf_op jit(solution)/shard_map/ppermute | solution.py:300
  66.2 3.2 %collective-permute-done.10.refs_6_ = bf16[128,256]{1,0:T(8,128)(2,1)S(1)} collective-permute-done((bf16[128,256]{1,0:T(8,128)(2,1)S(1)}, bf16[128,256]{1,0:T(8,128)(2,1)S(1)}, u32[]{:S(2)}, u32[]{:S(2)}) %collective-permute-start.10) | collective-permute-done | bytes 65568 | tf_op jit(solution)/shard_map/ppermute | solution.py:300
  69.4 0.3 collective-permute-done.11.refs_7_
  69.7 0.8 %join.1 = bf16[128,2048]{1,0:T(8,128)(2,1)} custom-call(bf16[128,256]{1,0:T(8,128)(2,1)S(1)} %get-tuple-element.34.refs_0_, bf16[128,256]{1,0:T(8,128)(2,1)S(1)} %collective-permute-done.3.refs_1_, bf16[128,256]{1,0:T(8,128)(2,1)S(1)} %collective-permute-done.4.refs_2_, bf16[128,256]{1,0:T(8,128)(2,1)S(1)} %collective-permute-done.5.refs_3_, ...), custom_call_target="tpu_custom_call" | custom-call | tf_op jit(solution)/shard_map/join/pallas_call | solution.py:351
  (17 shorter events, 0.2 us)
Async XLA Ops:
  0.0 9.8 %copy-start = (s32[40,4]{0,1:T(4,128)S(1)}, s32[40,4]{0,1:T(4,128)}, u32[]{:S(2)}) copy-start(s32[40,4]{0,1:T(4,128)} %param.12) | copy-start | bytes 1924
  0.0 9.8 %copy-start.1 = (s32[4]{0:T(128)S(1)}, s32[4]{0:T(128)}, u32[]{:S(2)}) copy-start(s32[4]{0:T(128)} %parent.1) | copy-start | bytes 52
  0.0 9.8 %copy-start.2 = (s32[40]{0:T(128)S(1)}, s32[40]{0:T(128)}, u32[]{:S(2)}) copy-start(s32[40]{0:T(128)} %up.1) | copy-start | bytes 484
  3.6 45.9 %all-to-all-start = ((bf16[16,3,128,128]{3,2,1,0:T(8,128)(2,1)}), bf16[16,3,128,128]{3,2,1,0:T(8,128)(2,1)S(1)}, u32[]{:S(2)}, u32[]{:S(2)}) async-start(bf16[16,3,128,128]{3,2,1,0:T(8,128)(2,1)} %get-tuple-element.33), calls=%async_computation | async-start | bytes 3145728 | tf_op jit(solution)/shard_map/all_to_all | solution.py:302
  9.8 0.7 copy-start.3
  12.5 1.9 %collective-permute-start = (bf16[128,1536]{1,0:T(8,128)(2,1)S(1)}, bf16[128,1536]{1,0:T(8,128)(2,1)S(1)}, u32[]{:S(2)}, u32[]{:S(2)}) collective-permute-start(bf16[128,1536]{1,0:T(8,128)(2,1)S(1)} %get-tuple-element.30), channel_id=1, source_target_pairs={{0,1},{1,0},{2,3},{3,2},{4,5},{5,4},{6,7},{7,6},{8,9},{9,8},{10,11... | collective-permute-start | bytes 1179656 | tf_op jit(solution)/shard_map/ppermute | solution.py:300
  12.7 20.0 %collective-permute-start.1 = (bf16[128,1536]{1,0:T(8,128)(2,1)S(1)}, bf16[128,1536]{1,0:T(8,128)(2,1)S(1)}, u32[]{:S(2)}, u32[]{:S(2)}) collective-permute-start(bf16[128,1536]{1,0:T(8,128)(2,1)S(1)} %get-tuple-element.31), channel_id=1, source_target_pairs={{0,2},{1,3},{2,0},{3,1},{4,6},{5,7},{6,4},{7,5},{8,10},{9,11},{10,... | collective-permute-start | bytes 1179656 | tf_op jit(solution)/shard_map/ppermute | solution.py:300
  14.1 30.1 %collective-permute-start.2 = (bf16[128,1536]{1,0:T(8,128)(2,1)S(1)}, bf16[128,1536]{1,0:T(8,128)(2,1)S(1)}, u32[]{:S(2)}, u32[]{:S(2)}) collective-permute-start(bf16[128,1536]{1,0:T(8,128)(2,1)S(1)} %get-tuple-element.32), channel_id=1, source_target_pairs={{0,3},{1,2},{2,1},{3,0},{4,7},{5,6},{6,5},{7,4},{8,11},{9,10},{10,... | collective-permute-start | bytes 1179656 | tf_op jit(solution)/shard_map/ppermute | solution.py:300
  45.1 13.3 %collective-permute-start.6 = (bf16[4,128,128]{2,1,0:T(8,128)(2,1)}, bf16[4,128,128]{2,1,0:T(8,128)(2,1)S(1)}, u32[]{:S(2)}, u32[]{:S(2)}) collective-permute-start(bf16[4,128,128]{2,1,0:T(8,128)(2,1)} %get-tuple-element.42), channel_id=1, source_target_pairs={{0,4},{1,5},{2,6},{3,7},{4,0},{5,1},{6,2},{7,3},{8,12},{9,13},{10,... | collective-permute-start | bytes 393224 | tf_op jit(solution)/shard_map/ppermute | solution.py:300
  48.0 11.3 %collective-permute-start.7 = (bf16[4,128,128]{2,1,0:T(8,128)(2,1)}, bf16[4,128,128]{2,1,0:T(8,128)(2,1)S(1)}, u32[]{:S(2)}, u32[]{:S(2)}) collective-permute-start(bf16[4,128,128]{2,1,0:T(8,128)(2,1)} %get-tuple-element.43), channel_id=1, source_target_pairs={{0,8},{1,9},{2,10},{3,11},{4,12},{5,13},{6,14},{7,15},{8,0},{9,1},... | collective-permute-start | bytes 393224 | tf_op jit(solution)/shard_map/ppermute | solution.py:300
  48.4 13.7 %collective-permute-start.8 = (bf16[4,128,128]{2,1,0:T(8,128)(2,1)}, bf16[4,128,128]{2,1,0:T(8,128)(2,1)}, u32[]{:S(2)}, u32[]{:S(2)}) collective-permute-start(bf16[4,128,128]{2,1,0:T(8,128)(2,1)} %get-tuple-element.44), channel_id=1, source_target_pairs={{0,12},{1,13},{2,14},{3,15},{4,8},{5,9},{6,10},{7,11},{8,4},{9,5},... | collective-permute-start | bytes 393224 | tf_op jit(solution)/shard_map/ppermute | solution.py:300
  53.8 11.2 %collective-permute-start.3 = (bf16[128,256]{1,0:T(8,128)(2,1)S(1)}, bf16[128,256]{1,0:T(8,128)(2,1)S(1)}, u32[]{:S(2)}, u32[]{:S(2)}) collective-permute-start(bf16[128,256]{1,0:T(8,128)(2,1)S(1)} %get-tuple-element.35), channel_id=1, source_target_pairs={{0,1},{1,0},{2,3},{3,2},{4,5},{5,4},{6,7},{7,6},{8,9},{9,8},{10,11... | collective-permute-start | bytes 196616 | tf_op jit(solution)/shard_map/ppermute | solution.py:300
  53.9 12.3 %collective-permute-start.4 = (bf16[128,256]{1,0:T(8,128)(2,1)S(1)}, bf16[128,256]{1,0:T(8,128)(2,1)S(1)}, u32[]{:S(2)}, u32[]{:S(2)}) collective-permute-start(bf16[128,256]{1,0:T(8,128)(2,1)S(1)} %get-tuple-element.36), channel_id=1, source_target_pairs={{0,2},{1,3},{2,0},{3,1},{4,6},{5,7},{6,4},{7,5},{8,10},{9,11},{10,... | collective-permute-start | bytes 196616 | tf_op jit(solution)/shard_map/ppermute | solution.py:300
  58.4 7.8 %collective-permute-start.5 = (bf16[128,256]{1,0:T(8,128)(2,1)S(1)}, bf16[128,256]{1,0:T(8,128)(2,1)S(1)}, u32[]{:S(2)}, u32[]{:S(2)}) collective-permute-start(bf16[128,256]{1,0:T(8,128)(2,1)S(1)} %get-tuple-element.37), channel_id=1, source_target_pairs={{0,3},{1,2},{2,1},{3,0},{4,7},{5,6},{6,5},{7,4},{8,11},{9,10},{10,... | collective-permute-start | bytes 196616 | tf_op jit(solution)/shard_map/ppermute | solution.py:300
  64.3 1.9 %collective-permute-start.9 = (bf16[128,256]{1,0:T(8,128)(2,1)S(1)}, bf16[128,256]{1,0:T(8,128)(2,1)S(1)}, u32[]{:S(2)}, u32[]{:S(2)}) collective-permute-start(bf16[128,256]{1,0:T(8,128)(2,1)S(1)} %get-tuple-element.46), channel_id=1, source_target_pairs={{0,1},{1,0},{2,3},{3,2},{4,5},{5,4},{6,7},{7,6},{8,9},{9,8},{10,11... | collective-permute-start | bytes 196616 | tf_op jit(solution)/shard_map/ppermute | solution.py:300
  64.4 5.0 %collective-permute-start.10 = (bf16[128,256]{1,0:T(8,128)(2,1)S(1)}, bf16[128,256]{1,0:T(8,128)(2,1)S(1)}, u32[]{:S(2)}, u32[]{:S(2)}) collective-permute-start(bf16[128,256]{1,0:T(8,128)(2,1)S(1)} %get-tuple-element.47), channel_id=1, source_target_pairs={{0,2},{1,3},{2,0},{3,1},{4,6},{5,7},{6,4},{7,5},{8,10},{9,11},{10,... | collective-permute-start | bytes 196616 | tf_op jit(solution)/shard_map/ppermute | solution.py:300
  65.0 4.7 %collective-permute-start.11 = (bf16[128,256]{1,0:T(8,128)(2,1)S(1)}, bf16[128,256]{1,0:T(8,128)(2,1)S(1)}, u32[]{:S(2)}, u32[]{:S(2)}) collective-permute-start(bf16[128,256]{1,0:T(8,128)(2,1)S(1)} %get-tuple-element.48), channel_id=1, source_target_pairs={{0,3},{1,2},{2,1},{3,0},{4,7},{5,6},{6,5},{7,4},{8,11},{9,10},{10,... | collective-permute-start | bytes 196616 | tf_op jit(solution)/shard_map/ppermute | solution.py:300

commit v3 on v2

v3 whole, which is shorter than its diff:
```python
import jax
import jax.numpy as jnp
from jax import lax
from jax.experimental import pallas as pl
from jax.experimental.pallas import tpu as pltpu
from jax.sharding import PartitionSpec as P


HEADS = 16
KV_HEADS = 8
HEAD_DIM = 128
DEPTHS = 4
MEMBERS = 4
GROUP = HEADS // KV_HEADS
KV_COLS = KV_HEADS // MEMBERS * HEAD_DIM
OWN_COLS = HEADS // MEMBERS * HEAD_DIM + 2 * KV_COLS
STAGE_VMEM = 60 * 1024 * 2**10
PIECES_VMEM = 52 * 2**20

query_scale = 168.0 ** (-0.5)
exp2_scale = query_scale * 1.4426950408889634


def dot_t(a, b):
    return lax.dot_general(a, b, (((1,), (1,)), ((), ())), preferred_element_type=jnp.float32)


def dot(a, b):
    return lax.dot_general(a, b, (((1,), (0,)), ((), ())), preferred_element_type=jnp.float32)


def walk(parent, up, g):
    out = [parent[g]]
    for _ in range(DEPTHS - 1):
        out.append(jnp.where(out[-1] >= 0, up[jnp.maximum(out[-1], 0)], -1))
    return out


HEADS_HERE = KV_HEADS // MEMBERS


def stage_kernel(parent_in, up_in, owner_in, slot_in, store, send, picks, parent, up, owner, slot, sems):
    tables = ((parent_in, parent), (up_in, up), (owner_in, owner), (slot_in, slot))
    copies = [pltpu.make_async_copy(src, dst, sems.at[i]) for i, (src, dst) in enumerate(tables)]
    for c in copies:
        c.start()
    me = lax.axis_index("nodes")
    segs = parent.shape[0]
    blocks = owner.shape[1]
    sem = sems.at[len(copies)]
    for c in copies:
        c.wait()
    pick_of = jnp.max(jnp.where(owner[...] == me, slot[...], 0), axis=0, keepdims=True)
    lanes = lax.broadcasted_iota(jnp.int32, (1, blocks), 1)

    def one_segment(g, carry):
        on_path = lanes < 0
        for block in walk(parent, up, g):
            on_path = on_path | (lanes == block)
        pick = jnp.max(jnp.where(on_path, pick_of, 0))
        picks[g] = pick
        for m in range(MEMBERS):
            src = store.at[0, pick, :, pl.ds(m * KV_COLS, KV_COLS)]
            pltpu.make_async_copy(src, send.at[g * MEMBERS + m], sem).start()
        return carry

    lax.fori_loop(0, segs, one_segment, 0, unroll=segs <= 4)
    pltpu.make_async_copy(send, send, sem).wait()


def pieces_kernel(parent, up, owner, picks, queries, seg_kv, store, bias, *rest):
    owns, late, sems = rest[:MEMBERS], rest[MEMBERS:-1], rest[-1]
    me = lax.axis_index("nodes")
    member = me % MEMBERS
    page_tok = store.shape[2]
    q_cols = queries.shape[1] // MEMBERS
    kv_cols = seg_kv.shape[2] // MEMBERS
    for d in range(MEMBERS):
        to = member ^ d
        q_at = pl.multiple_of(to * q_cols, q_cols)
        kv_at = pl.multiple_of(to * kv_cols, kv_cols)
        sem = sems.at[d]
        pltpu.make_async_copy(queries.at[:, pl.ds(q_at, q_cols)], owns[d].at[:, pl.ds(0, q_cols)], sem).start()
        for i in range(2):
            pltpu.make_async_copy(
                seg_kv.at[i, :, pl.ds(kv_at, kv_cols)], owns[d].at[:, pl.ds(q_cols + i * kv_cols, kv_cols)], sem
            ).start()
    for d, ref in enumerate(late):
        to = me ^ d
        at = pl.multiple_of(to % MEMBERS * KV_COLS, KV_COLS)
        pltpu.make_async_copy(
            store.at[1, picks[to // MEMBERS], :, pl.ds(at, KV_COLS)], ref, sems.at[MEMBERS + d]
        ).start()
    page_bias(parent, up, owner, bias, page_tok)
    for i, ref in enumerate((*owns, *late)):
        pltpu.make_async_copy(ref, ref, sems.at[i]).wait()


def page_bias(parent, up, owner, bias_ref, page_tok):
    pages, blocks = owner.shape
    path = walk(parent, up, lax.axis_index("nodes") // MEMBERS)
    rows = lax.broadcasted_iota(jnp.int32, (8, blocks), 0)
    block_at = jnp.full((8, blocks), -1, jnp.int32)
    for i, block in enumerate(path):
        block_at = jnp.where(rows == i, block, block_at)
    chosen = (lax.broadcasted_iota(jnp.int32, (8, blocks), 1) == block_at).astype(jnp.float32)
    above = owner[...].astype(jnp.float32) + 1.0
    held_by = lax.dot_general(
        chosen, above, (((1,), (1,)), ((), ())), precision=lax.Precision.HIGHEST, preferred_element_type=jnp.float32
    )
    held_by = (held_by + 0.5).astype(jnp.int32) - 1
    for at in range(0, bias_ref.shape[1], 128):
        page = (lax.broadcasted_iota(jnp.int32, (8, 128), 1) + at) // page_tok
        found = jnp.zeros((8, 128), jnp.float32)
        for p in range(pages):
            found = jnp.where(held_by[:, p : p + 1] == page, 1.0, found)
        found = jnp.max(found, axis=0, keepdims=True)
        bias_ref[:, at : at + 128] = jnp.where(found > 0.0, 0.0, -jnp.inf)


def head_inputs(pieces, h):
    q_cols, kv_cols = GROUP * KV_COLS, KV_COLS
    q, k, v = [], [], []
    for piece in pieces:
        at = h * GROUP * HEAD_DIM
        q.append([piece[:, at + i * HEAD_DIM : at + (i + 1) * HEAD_DIM] for i in range(GROUP)])
        at = q_cols + h * HEAD_DIM
        k.append(piece[:, at : at + HEAD_DIM])
        v.append(piece[:, at + kv_cols : at + kv_cols + HEAD_DIM])
    queries = [jnp.concatenate(one, axis=0) for one in q]
    return queries, jnp.concatenate(k, axis=0), jnp.concatenate(v, axis=0)


def own_mask(member, d, rows, tok):
    cols = MEMBERS * tok
    r = lax.broadcasted_iota(jnp.int32, (rows, cols), 0)
    c = lax.broadcasted_iota(jnp.int32, (rows, cols), 1)
    q_at = (member ^ d) * tok + r % tok
    k_at = (member ^ (c // tok)) * tok + c % tok
    return k_at <= q_at


def softmax_parts(q, k_own, k_pages, bias_ref, score_ref, visible, step):
    keys = k_pages.shape[0]
    own = jnp.where(visible, dot_t(q, k_own), -jnp.inf)
    top = jnp.max(own, axis=1, keepdims=True)
    for at in range(0, keys, step):
        s = dot_t(q, k_pages[at : at + step]) + bias_ref[:, at : at + step]
        score_ref[:, at : at + step] = s
        top = jnp.maximum(top, jnp.max(s, axis=1, keepdims=True))
    top = top * exp2_scale
    own = jnp.exp2(own * exp2_scale - top)
    return own, top


def weights_kernel(bias_ref, p0, p1, p2, p3, pages, *rest):
    results, score_ref = rest[:-1], rest[-1]
    member = lax.axis_index("nodes") % MEMBERS
    tok = p0.shape[0]
    keys = bias_ref.shape[1]
    step = min(keys, 512)
    for h in range(HEADS_HERE):
        w_ref, mixed_ref, total_ref = results[3 * h : 3 * h + 3]
        queries, k_own, v_own = head_inputs((p0, p1, p2, p3), h)
        k_pages = pages[:, :, h * HEAD_DIM : (h + 1) * HEAD_DIM].reshape(keys, HEAD_DIM)
        for d in range(MEMBERS):
            visible = own_mask(member, d, GROUP * tok, tok)
            own, top = softmax_parts(queries[d], k_own, k_pages, bias_ref, score_ref, visible, step)
            total = jnp.sum(own, axis=1, keepdims=True)
            mixed_ref[d] = dot(own.astype(jnp.bfloat16), v_own)
            for at in range(0, keys, step):
                w = jnp.exp2(score_ref[:, at : at + step] * exp2_scale - top)
                total = total + jnp.sum(w, axis=1, keepdims=True)
                w_ref[d, :, at : at + step] = w.astype(jnp.bfloat16)
            total_ref[d] = jnp.broadcast_to(total, total_ref.shape[1:])


def values_kernel(h, w_ref, mixed_ref, total_ref, *rest):
    late, outs, v_ref = rest[: -MEMBERS - 1], rest[-MEMBERS - 1 : -1], rest[-1]
    me = lax.axis_index("nodes")
    tok = outs[0].shape[0]
    rows = late[0].shape[0]
    for d, ref in enumerate(late):
        v_ref[pl.ds(pl.multiple_of((me ^ d) * rows, rows), rows)] = ref[:, h * HEAD_DIM : (h + 1) * HEAD_DIM]
    for d, out in enumerate(outs):
        mixed = mixed_ref[d] + dot(w_ref[d], v_ref[...])
        res = (mixed / total_ref[d]).astype(jnp.bfloat16)
        for i in range(GROUP):
            out[:, i * HEAD_DIM : (i + 1) * HEAD_DIM] = res[i * tok : (i + 1) * tok]


def join_kernel(*refs):
    parts, out, sems = refs[:8], refs[8], refs[9]
    member = lax.axis_index("nodes") % MEMBERS
    width = parts[0].shape[1]
    copies = []
    for h in range(2):
        for d in range(MEMBERS):
            at = pl.multiple_of(((member ^ d) * 2 + h) * width, width)
            i = h * MEMBERS + d
            copies.append(pltpu.make_async_copy(parts[i], out.at[:, pl.ds(at, width)], sems.at[i]))
    for c in copies:
        c.start()
    for c in copies:
        c.wait()


def local(queries, seg_kv, kv_store, seg_parent, block_up, page_owner, page_slot):
    nodes = lax.axis_size("nodes")
    segs = nodes // MEMBERS
    tok = queries.shape[0]
    page_tok = kv_store.shape[2]
    keys = nodes * page_tok
    bf16, f32, i32 = jnp.bfloat16, jnp.float32, jnp.int32
    hbm = pl.BlockSpec(memory_space=pltpu.HBM)
    smem = pl.BlockSpec(memory_space=pltpu.SMEM)
    vmem = pl.BlockSpec(memory_space=pltpu.VMEM)
    params = pltpu.CompilerParams(vmem_limit_bytes=24 * 2**20)
    wide = pltpu.CompilerParams(vmem_limit_bytes=STAGE_VMEM)
    own = jax.ShapeDtypeStruct((tok, OWN_COLS), bf16)
    early = jax.ShapeDtypeStruct((nodes, page_tok, KV_COLS), bf16)
    late = jax.ShapeDtypeStruct((page_tok, KV_COLS), bf16)
    owner_of, slot_of = page_owner.T, page_slot.T
    send, picks = pl.pallas_call(
        stage_kernel,
        in_specs=[hbm] * 5,
        out_specs=[vmem, smem],
        out_shape=[early, jax.ShapeDtypeStruct((segs,), i32)],
        scratch_shapes=[
            pltpu.SMEM(seg_parent.shape, i32),
            pltpu.SMEM(block_up.shape, i32),
            pltpu.VMEM(owner_of.shape, i32),
            pltpu.VMEM(slot_of.shape, i32),
            pltpu.SemaphoreType.DMA((5,)),
        ],
        compiler_params=wide,
        name="stage",
    )(seg_parent, block_up, owner_of, slot_of, kv_store)
    got = lax.all_to_all(send, "nodes", split_axis=0, concat_axis=0, tiled=True)
    bias, *staged = pl.pallas_call(
        pieces_kernel,
        in_specs=[smem] * 2 + [vmem] + [smem] + [hbm] * 3,
        out_specs=[vmem] * (1 + MEMBERS + nodes),
        out_shape=[jax.ShapeDtypeStruct((1, keys), f32)] + [own] * MEMBERS + [late] * nodes,
        scratch_shapes=[pltpu.SemaphoreType.DMA((MEMBERS + nodes,))],
        compiler_params=pltpu.CompilerParams(vmem_limit_bytes=PIECES_VMEM),
        name="pieces",
    )(seg_parent, block_up, owner_of, picks, queries, seg_kv, kv_store)
    owns, held = staged[:MEMBERS], staged[MEMBERS:]

    def swapped(x, d):
        return lax.ppermute(x, "nodes", [(i, i ^ d) for i in range(nodes)])

    pieces = [owns[0]] + [swapped(owns[d], d) for d in range(1, MEMBERS)]
    values = [held[0]] + [swapped(held[d], d) for d in range(1, nodes)]
    rows = GROUP * tok
    out_piece = jax.ShapeDtypeStruct((tok, GROUP * HEAD_DIM), bf16)
    sums = jax.ShapeDtypeStruct((MEMBERS, rows, HEAD_DIM), f32)
    results = pl.pallas_call(
        lambda *refs: weights_kernel(*refs),
        in_specs=[vmem] * (2 + MEMBERS),
        out_specs=[vmem] * (3 * HEADS_HERE),
        out_shape=[jax.ShapeDtypeStruct((MEMBERS, rows, keys), bf16), sums, sums] * HEADS_HERE,
        scratch_shapes=[pltpu.VMEM((rows, keys), f32)],
        compiler_params=params,
        name="weights",
    )(bias, *pieces, got)
    parts = []
    for h in range(HEADS_HERE):
        one = pl.pallas_call(
            lambda *refs, h=h: values_kernel(h, *refs),
            in_specs=[vmem] * (3 + nodes),
            out_specs=[vmem] * MEMBERS,
            out_shape=[out_piece] * MEMBERS,
            scratch_shapes=[pltpu.VMEM((keys, HEAD_DIM), bf16)],
            compiler_params=params,
        )(*results[3 * h : 3 * h + 3], *values)
        parts += [one[0]] + [swapped(one[d], d) for d in range(1, MEMBERS)]
    return pl.pallas_call(
        join_kernel,
        in_specs=[vmem] * 8,
        out_specs=hbm,
        out_shape=jax.ShapeDtypeStruct(queries.shape, bf16),
        scratch_shapes=[pltpu.SemaphoreType.DMA((8,))],
        compiler_params=params,
        name="join",
    )(*parts)


def solution(mesh):
    in_specs = (
        P(("groups", "nodes"), None),
        P(None, ("groups", "nodes"), None),
        P(None, ("groups", "nodes"), None, None),
        P("groups"),
        P("groups"),
        P("groups", None),
        P("groups", None),
    )
    out_specs = P(("groups", "nodes"), None)

    return jax.shard_map(local, mesh=mesh, in_specs=in_specs, out_specs=out_specs, check_vma=False)
```

time: 71.9 us -> 79.3 us (1.10)
  the two profiles are of different devices: /device:TPU:16 before, /device:TPU:1 now
where the time goes in v3:
time: 79.3 us; the launch traced here: 78.9 us
  starting transfers between devices  46.1 us (58%)
  Pallas kernels  17 us (21%)
  waiting for transfers between devices  15 us (19%)
    ppermute x24, starting transfers between devices, swapped(): return lax.ppermute(x, 'nodes', [(i, i ^ d) for i in range(nodes)])  38.9 us
    ppermute x24, waiting for transfers between devices, swapped(): return lax.ppermute(x, 'nodes', [(i, i ^ d) for i in range(nodes)])  15 us
    all_to_all x1, starting transfers between devices, local(): got = lax.all_to_all(send, 'nodes', split_axis=0, concat_axis=0, tiled=True)  7.2 us
    pallas_call x1, Pallas kernels, local(): pl.pallas_call(lambda *refs: weights_kernel(*refs), in_specs=[vmem] * (2...  6.92 us
    pallas_call x1, Pallas kernels, local(): pl.pallas_call(stage_kernel, in_specs=[hbm] * 5, out_specs=[vmem, smem],...  3.42 us
    pallas_call x1, Pallas kernels, local(): pl.pallas_call(pieces_kernel, in_specs=[smem] * 2 + [vmem] + [smem] + [hb...  3.08 us
    pallas_call x2, Pallas kernels, local(): pl.pallas_call(lambda *refs, h=h: values_kernel(h, *refs), in_specs=[vmem...  2.74 us
  transfers between devices with their start and end apart: 25, of which 7 were waited for; matrix products, arithmetic and copies ran while one was open for 0% of the time, Pallas kernels for 14%

profile of v3, /device:TPU:1, one launch (start us, length us, event | category | flops | bytes accessed | tf_op | source)
XLA Modules:
  0.0 78.9 jit_solution(7087624565449300538)
XLA Ops:
  0.0 3.4 %stage.1 = (bf16[16,128,256]{2,1,0:T(8,128)(2,1)}, s32[4]{0:T(128)}) custom-call(s32[4]{0:T(128)} %parent.1, s32[40]{0:T(128)} %up.1, s32[4,40]{1,0:T(4,128)} %bitcast.2, s32[4,40]{1,0:T(4,128)} %bitcast.4, bf16[2,27,128,1024]{3,2,1,0:T(8,128)(2,1)} %store.3), custom_call_target="tpu_custom_call" | custom-call | tf_op jit(solution)/shard_map/stage/pallas_call | solution.py:224
  3.4 7.2 %all-to-all-start = ((bf16[16,128,256]{2,1,0:T(8,128)(2,1)}), bf16[16,128,256]{2,1,0:T(8,128)(2,1)S(1)}, u32[]{:S(2)}, u32[]{:S(2)}) async-start(bf16[16,128,256]{2,1,0:T(8,128)(2,1)} %get-tuple-element.48), calls=%async_computation | async-start | bytes 2097152 | tf_op jit(solution)/shard_map/all_to_all | solution.py:239
  11.3 3.1 %pieces.1 = (f32[1,2048]{1,0:T(1,128)S(1)}, bf16[128,1024]{1,0:T(8,128)(2,1)S(1)}, bf16[128,1024]{1,0:T(8,128)(2,1)S(1)}, bf16[128,1024]{1,0:T(8,128)(2,1)S(1)},...) custom-call(s32[4]{0:T(128)S(1)} %copy-done.1, ...), custom_call_target="tpu_custom_call" | custom-call | tf_op jit(solution)/shard_map/pieces/pallas_call | solution.py:240
  14.6 1.6 %collective-permute-start.4 = (bf16[128,256]{1,0:T(8,128)(2,1)S(1)}, bf16[128,256]{1,0:T(8,128)(2,1)S(1)}, u32[]{:S(2)}, u32[]{:S(2)}) collective-permute-start(bf16[128,256]{1,0:T(8,128)(2,1)S(1)} %get-tuple-element.54), channel_id=1, source_target_pairs={{0,2},{1,3},{2,0},{3,1},{4,6},{5,7},{6,4},{7,5},{8,10},{9,11},{10,... | collective-permute-start | bytes 196616 | tf_op jit(solution)/shard_map/ppermute | solution.py:252
  19.8 3.0 %collective-permute-start.2 = (bf16[128,1024]{1,0:T(8,128)(2,1)}, bf16[128,1024]{1,0:T(8,128)(2,1)S(1)}, u32[]{:S(2)}, u32[]{:S(2)}) collective-permute-start(bf16[128,1024]{1,0:T(8,128)(2,1)} %get-tuple-element.47), channel_id=1, source_target_pairs={{0,3},{1,2},{2,1},{3,0},{4,7},{5,6},{6,5},{7,4},{8,11},{9,10},{10,... | collective-permute-start | bytes 786440 | tf_op jit(solution)/shard_map/ppermute | solution.py:252
  22.8 2.0 %collective-permute-done.5.refs_6_ = bf16[128,256]{1,0:T(8,128)(2,1)S(1)} collective-permute-done((bf16[128,256]{1,0:T(8,128)(2,1)S(1)}, bf16[128,256]{1,0:T(8,128)(2,1)S(1)}, u32[]{:S(2)}, u32[]{:S(2)}) %collective-permute-start.5) | collective-permute-done | bytes 65568 | tf_op jit(solution)/shard_map/ppermute | solution.py:252
  24.9 4.9 %collective-permute-done.6.refs_7_ = bf16[128,256]{1,0:T(8,128)(2,1)S(1)} collective-permute-done((bf16[128,256]{1,0:T(8,128)(2,1)S(1)}, bf16[128,256]{1,0:T(8,128)(2,1)S(1)}, u32[]{:S(2)}, u32[]{:S(2)}) %collective-permute-start.6) | collective-permute-done | bytes 65568 | tf_op jit(solution)/shard_map/ppermute | solution.py:252
  29.8 2.6 %collective-permute-start.8 = (bf16[128,256]{1,0:T(8,128)(2,1)S(1)}, bf16[128,256]{1,0:T(8,128)(2,1)S(1)}, u32[]{:S(2)}, u32[]{:S(2)}) collective-permute-start(bf16[128,256]{1,0:T(8,128)(2,1)S(1)} %get-tuple-element.58), channel_id=1, source_target_pairs={{0,6},{1,7},{2,4},{3,5},{4,2},{5,3},{6,0},{7,1},{8,14},{9,15},{10,... | collective-permute-start | bytes 196616 | tf_op jit(solution)/shard_map/ppermute | solution.py:252
  32.4 1.7 %collective-permute-start.9 = (bf16[128,256]{1,0:T(8,128)(2,1)S(1)}, bf16[128,256]{1,0:T(8,128)(2,1)S(1)}, u32[]{:S(2)}, u32[]{:S(2)}) collective-permute-start(bf16[128,256]{1,0:T(8,128)(2,1)S(1)} %get-tuple-element.59), channel_id=1, source_target_pairs={{0,7},{1,6},{2,5},{3,4},{4,3},{5,2},{6,1},{7,0},{8,15},{9,14},{10,... | collective-permute-start | bytes 196616 | tf_op jit(solution)/shard_map/ppermute | solution.py:252
  34.1 1.8 %collective-permute-done.8.refs_9_ = bf16[128,256]{1,0:T(8,128)(2,1)S(1)} collective-permute-done((bf16[128,256]{1,0:T(8,128)(2,1)S(1)}, bf16[128,256]{1,0:T(8,128)(2,1)S(1)}, u32[]{:S(2)}, u32[]{:S(2)}) %collective-permute-start.8) | collective-permute-done | bytes 65568 | tf_op jit(solution)/shard_map/ppermute | solution.py:252
  35.9 2.2 %collective-permute-start.10 = (bf16[128,256]{1,0:T(8,128)(2,1)S(1)}, bf16[128,256]{1,0:T(8,128)(2,1)S(1)}, u32[]{:S(2)}, u32[]{:S(2)}) collective-permute-start(bf16[128,256]{1,0:T(8,128)(2,1)S(1)} %get-tuple-element.60), channel_id=1, source_target_pairs={{0,8},{1,9},{2,10},{3,11},{4,12},{5,13},{6,14},{7,15},{8,0},{9,1},... | collective-permute-start | bytes 196616 | tf_op jit(solution)/shard_map/ppermute | solution.py:252
  38.0 2.5 %collective-permute-start.11 = (bf16[128,256]{1,0:T(8,128)(2,1)S(1)}, bf16[128,256]{1,0:T(8,128)(2,1)S(1)}, u32[]{:S(2)}, u32[]{:S(2)}) collective-permute-start(bf16[128,256]{1,0:T(8,128)(2,1)S(1)} %get-tuple-element.61), channel_id=1, source_target_pairs={{0,9},{1,8},{2,11},{3,10},{4,13},{5,12},{6,15},{7,14},{8,1},{9,0},... | collective-permute-start | bytes 196616 | tf_op jit(solution)/shard_map/ppermute | solution.py:252
  40.5 3.4 %collective-permute-start.12 = (bf16[128,256]{1,0:T(8,128)(2,1)S(1)}, bf16[128,256]{1,0:T(8,128)(2,1)S(1)}, u32[]{:S(2)}, u32[]{:S(2)}) collective-permute-start(bf16[128,256]{1,0:T(8,128)(2,1)S(1)} %get-tuple-element.62), channel_id=1, source_target_pairs={{0,10},{1,11},{2,8},{3,9},{4,14},{5,15},{6,12},{7,13},{8,2},{9,3},... | collective-permute-start | bytes 196616 | tf_op jit(solution)/shard_map/ppermute | solution.py:252
  44.0 2.9 %collective-permute-done.11.refs_12_ = bf16[128,256]{1,0:T(8,128)(2,1)S(1)} collective-permute-done((bf16[128,256]{1,0:T(8,128)(2,1)S(1)}, bf16[128,256]{1,0:T(8,128)(2,1)S(1)}, u32[]{:S(2)}, u32[]{:S(2)}) %collective-permute-start.11) | collective-permute-done | bytes 65568 | tf_op jit(solution)/shard_map/ppermute | solution.py:252
  46.9 2.0 %collective-permute-start.13 = (bf16[128,256]{1,0:T(8,128)(2,1)S(1)}, bf16[128,256]{1,0:T(8,128)(2,1)S(1)}, u32[]{:S(2)}, u32[]{:S(2)}) collective-permute-start(bf16[128,256]{1,0:T(8,128)(2,1)S(1)} %get-tuple-element.63), channel_id=1, source_target_pairs={{0,11},{1,10},{2,9},{3,8},{4,15},{5,14},{6,13},{7,12},{8,3},{9,2},... | collective-permute-start | bytes 196616 | tf_op jit(solution)/shard_map/ppermute | solution.py:252
  48.9 2.2 %collective-permute-start.14 = (bf16[128,256]{1,0:T(8,128)(2,1)S(1)}, bf16[128,256]{1,0:T(8,128)(2,1)S(1)}, u32[]{:S(2)}, u32[]{:S(2)}) collective-permute-start(bf16[128,256]{1,0:T(8,128)(2,1)S(1)} %get-tuple-element.64), channel_id=1, source_target_pairs={{0,12},{1,13},{2,14},{3,15},{4,8},{5,9},{6,10},{7,11},{8,4},{9,5},... | collective-permute-start | bytes 196616 | tf_op jit(solution)/shard_map/ppermute | solution.py:252
  51.1 5.5 %collective-permute-start.15 = (bf16[128,256]{1,0:T(8,128)(2,1)S(1)}, bf16[128,256]{1,0:T(8,128)(2,1)S(1)}, u32[]{:S(2)}, u32[]{:S(2)}) collective-permute-start(bf16[128,256]{1,0:T(8,128)(2,1)S(1)} %get-tuple-element.65), channel_id=1, source_target_pairs={{0,13},{1,12},{2,15},{3,14},{4,9},{5,8},{6,11},{7,10},{8,5},{9,4},... | collective-permute-start | bytes 196616 | tf_op jit(solution)/shard_map/ppermute | solution.py:252
  57.6 6.9 %weights.1 = (bf16[4,256,2048]{2,1,0:T(8,128)(2,1)S(1)}, f32[4,256,128]{2,1,0:T(8,128)S(1)}, f32[4,256,128]{2,1,0:T(8,128)S(1)}, bf16[4,256,2048]{2,1,0:T(8,128)...) custom-call(f32[1,2048]{1,0:T(1,128)S(1)} %get-tuple-element.43.refs_0_, ...), custom_call_target="tpu_custom_call" | custom-call | tf_op jit(solution)/shard_map/weights/pallas_call | solution.py:259
  64.5 1.4 %shard_map.73 = (bf16[128,256]{1,0:T(8,128)(2,1)S(1)}, bf16[128,256]{1,0:T(8,128)(2,1)S(1)}, bf16[128,256]{1,0:T(8,128)(2,1)S(1)}, bf16[128,256]{1,0:T(8,128)(2,1)S(1)}) custom-call(bf16[4,256,2048]{2,1,0:T(8,128)(2,1)S(1)} %get-tuple-element.49.refs_0_, f32[4,256,128]{2,1,0:T(8,128)S(1)} %get-tuple-element.50.refs_1_, ...), custom_call_target="tpu_custom_call" | custom-call | tf_op jit(solution)/shard_map/pallas_call | solution.py:270
  65.9 3.6 %collective-permute-start.18 = (bf16[128,256]{1,0:T(8,128)(2,1)S(1)}, bf16[128,256]{1,0:T(8,128)(2,1)S(1)}, u32[]{:S(2)}, u32[]{:S(2)}) collective-permute-start(bf16[128,256]{1,0:T(8,128)(2,1)S(1)} %get-tuple-element.69), channel_id=1, source_target_pairs={{0,1},{1,0},{2,3},{3,2},{4,5},{5,4},{6,7},{7,6},{8,9},{9,8},{10,11... | collective-permute-start | bytes 196616 | tf_op jit(solution)/shard_map/ppermute | solution.py:252
  69.6 1.7 %collective-permute-start.20 = (bf16[128,256]{1,0:T(8,128)(2,1)S(1)}, bf16[128,256]{1,0:T(8,128)(2,1)S(1)}, u32[]{:S(2)}, u32[]{:S(2)}) collective-permute-start(bf16[128,256]{1,0:T(8,128)(2,1)S(1)} %get-tuple-element.71), channel_id=1, source_target_pairs={{0,3},{1,2},{2,1},{3,0},{4,7},{5,6},{6,5},{7,4},{8,11},{9,10},{10,... | collective-permute-start | bytes 196616 | tf_op jit(solution)/shard_map/ppermute | solution.py:252
  71.3 1.4 %shard_map.74 = (bf16[128,256]{1,0:T(8,128)(2,1)S(1)}, bf16[128,256]{1,0:T(8,128)(2,1)S(1)}, bf16[128,256]{1,0:T(8,128)(2,1)S(1)}, bf16[128,256]{1,0:T(8,128)(2,1)S(1)}) custom-call(bf16[4,256,2048]{2,1,0:T(8,128)(2,1)S(1)} %get-tuple-element.72.refs_0_, f32[4,256,128]{2,1,0:T(8,128)S(1)} %get-tuple-element.73.refs_1_, ...), custom_call_target="tpu_custom_call" | custom-call | tf_op jit(solution)/shard_map/pallas_call | solution.py:270
  72.9 2.0 %collective-permute-start.23 = (bf16[128,256]{1,0:T(8,128)(2,1)S(1)}, bf16[128,256]{1,0:T(8,128)(2,1)S(1)}, u32[]{:S(2)}, u32[]{:S(2)}) collective-permute-start(bf16[128,256]{1,0:T(8,128)(2,1)S(1)} %get-tuple-element.78), channel_id=1, source_target_pairs={{0,3},{1,2},{2,1},{3,0},{4,7},{5,6},{6,5},{7,4},{8,11},{9,10},{10,... | collective-permute-start | bytes 196616 | tf_op jit(solution)/shard_map/ppermute | solution.py:252
  76.0 2.1 %collective-permute-done.23.refs_7_ = bf16[128,256]{1,0:T(8,128)(2,1)S(1)} collective-permute-done((bf16[128,256]{1,0:T(8,128)(2,1)S(1)}, bf16[128,256]{1,0:T(8,128)(2,1)S(1)}, u32[]{:S(2)}, u32[]{:S(2)}) %collective-permute-start.23) | collective-permute-done | bytes 65568 | tf_op jit(solution)/shard_map/ppermute | solution.py:252
  (40 shorter events, 7.6 us)
Async XLA Ops:
  3.4 54.1 %all-to-all-start = ((bf16[16,128,256]{2,1,0:T(8,128)(2,1)}), bf16[16,128,256]{2,1,0:T(8,128)(2,1)S(1)}, u32[]{:S(2)}, u32[]{:S(2)}) async-start(bf16[16,128,256]{2,1,0:T(8,128)(2,1)} %get-tuple-element.48), calls=%async_computation | async-start | bytes 2097152 | tf_op jit(solution)/shard_map/all_to_all | solution.py:239
  14.4 4.0 %collective-permute-start.3 = (bf16[128,256]{1,0:T(8,128)(2,1)S(1)}, bf16[128,256]{1,0:T(8,128)(2,1)S(1)}, u32[]{:S(2)}, u32[]{:S(2)}) collective-permute-start(bf16[128,256]{1,0:T(8,128)(2,1)S(1)} %get-tuple-element.53), channel_id=1, source_target_pairs={{0,1},{1,0},{2,3},{3,2},{4,5},{5,4},{6,7},{7,6},{8,9},{9,8},{10,11... | collective-permute-start | bytes 196616 | tf_op jit(solution)/shard_map/ppermute | solution.py:252
  14.6 5.2 %collective-permute-start.4 = (bf16[128,256]{1,0:T(8,128)(2,1)S(1)}, bf16[128,256]{1,0:T(8,128)(2,1)S(1)}, u32[]{:S(2)}, u32[]{:S(2)}) collective-permute-start(bf16[128,256]{1,0:T(8,128)(2,1)S(1)} %get-tuple-element.54), channel_id=1, source_target_pairs={{0,2},{1,3},{2,0},{3,1},{4,6},{5,7},{6,4},{7,5},{8,10},{9,11},{10,... | collective-permute-start | bytes 196616 | tf_op jit(solution)/shard_map/ppermute | solution.py:252
  16.2 8.6 %collective-permute-start.5 = (bf16[128,256]{1,0:T(8,128)(2,1)S(1)}, bf16[128,256]{1,0:T(8,128)(2,1)S(1)}, u32[]{:S(2)}, u32[]{:S(2)}) collective-permute-start(bf16[128,256]{1,0:T(8,128)(2,1)S(1)} %get-tuple-element.55), channel_id=1, source_target_pairs={{0,3},{1,2},{2,1},{3,0},{4,7},{5,6},{6,5},{7,4},{8,11},{9,10},{10,... | collective-permute-start | bytes 196616 | tf_op jit(solution)/shard_map/ppermute | solution.py:252
  16.6 13.1 %collective-permute-start.6 = (bf16[128,256]{1,0:T(8,128)(2,1)S(1)}, bf16[128,256]{1,0:T(8,128)(2,1)S(1)}, u32[]{:S(2)}, u32[]{:S(2)}) collective-permute-start(bf16[128,256]{1,0:T(8,128)(2,1)S(1)} %get-tuple-element.56), channel_id=1, source_target_pairs={{0,4},{1,5},{2,6},{3,7},{4,0},{5,1},{6,2},{7,3},{8,12},{9,13},{10,... | collective-permute-start | bytes 196616 | tf_op jit(solution)/shard_map/ppermute | solution.py:252
  18.0 33.1 %collective-permute-start = (bf16[128,1024]{1,0:T(8,128)(2,1)S(1)}, bf16[128,1024]{1,0:T(8,128)(2,1)S(1)}, u32[]{:S(2)}, u32[]{:S(2)}) collective-permute-start(bf16[128,1024]{1,0:T(8,128)(2,1)S(1)} %get-tuple-element.45), channel_id=1, source_target_pairs={{0,1},{1,0},{2,3},{3,2},{4,5},{5,4},{6,7},{7,6},{8,9},{9,8},{10,11... | collective-permute-start | bytes 786440 | tf_op jit(solution)/shard_map/ppermute | solution.py:252
  18.4 38.2 %collective-permute-start.1 = (bf16[128,1024]{1,0:T(8,128)(2,1)S(1)}, bf16[128,1024]{1,0:T(8,128)(2,1)S(1)}, u32[]{:S(2)}, u32[]{:S(2)}) collective-permute-start(bf16[128,1024]{1,0:T(8,128)(2,1)S(1)} %get-tuple-element.46), channel_id=1, source_target_pairs={{0,2},{1,3},{2,0},{3,1},{4,6},{5,7},{6,4},{7,5},{8,10},{9,11},{10,... | collective-permute-start | bytes 786440 | tf_op jit(solution)/shard_map/ppermute | solution.py:252
  19.8 36.8 %collective-permute-start.2 = (bf16[128,1024]{1,0:T(8,128)(2,1)}, bf16[128,1024]{1,0:T(8,128)(2,1)S(1)}, u32[]{:S(2)}, u32[]{:S(2)}) collective-permute-start(bf16[128,1024]{1,0:T(8,128)(2,1)} %get-tuple-element.47), channel_id=1, source_target_pairs={{0,3},{1,2},{2,1},{3,0},{4,7},{5,6},{6,5},{7,4},{8,11},{9,10},{10,... | collective-permute-start | bytes 786440 | tf_op jit(solution)/shard_map/ppermute | solution.py:252
  24.9 7.5 %collective-permute-start.7 = (bf16[128,256]{1,0:T(8,128)(2,1)S(1)}, bf16[128,256]{1,0:T(8,128)(2,1)S(1)}, u32[]{:S(2)}, u32[]{:S(2)}) collective-permute-start(bf16[128,256]{1,0:T(8,128)(2,1)S(1)} %get-tuple-element.57), channel_id=1, source_target_pairs={{0,5},{1,4},{2,7},{3,6},{4,1},{5,0},{6,3},{7,2},{8,13},{9,12},{10,... | collective-permute-start | bytes 196616 | tf_op jit(solution)/shard_map/ppermute | solution.py:252
  29.8 6.1 %collective-permute-start.8 = (bf16[128,256]{1,0:T(8,128)(2,1)S(1)}, bf16[128,256]{1,0:T(8,128)(2,1)S(1)}, u32[]{:S(2)}, u32[]{:S(2)}) collective-permute-start(bf16[128,256]{1,0:T(8,128)(2,1)S(1)} %get-tuple-element.58), channel_id=1, source_target_pairs={{0,6},{1,7},{2,4},{3,5},{4,2},{5,3},{6,0},{7,1},{8,14},{9,15},{10,... | collective-permute-start | bytes 196616 | tf_op jit(solution)/shard_map/ppermute | solution.py:252
  32.4 5.6 %collective-permute-start.9 = (bf16[128,256]{1,0:T(8,128)(2,1)S(1)}, bf16[128,256]{1,0:T(8,128)(2,1)S(1)}, u32[]{:S(2)}, u32[]{:S(2)}) collective-permute-start(bf16[128,256]{1,0:T(8,128)(2,1)S(1)} %get-tuple-element.59), channel_id=1, source_target_pairs={{0,7},{1,6},{2,5},{3,4},{4,3},{5,2},{6,1},{7,0},{8,15},{9,14},{10,... | collective-permute-start | bytes 196616 | tf_op jit(solution)/shard_map/ppermute | solution.py:252
  35.9 4.7 %collective-permute-start.10 = (bf16[128,256]{1,0:T(8,128)(2,1)S(1)}, bf16[128,256]{1,0:T(8,128)(2,1)S(1)}, u32[]{:S(2)}, u32[]{:S(2)}) collective-permute-start(bf16[128,256]{1,0:T(8,128)(2,1)S(1)} %get-tuple-element.60), channel_id=1, source_target_pairs={{0,8},{1,9},{2,10},{3,11},{4,12},{5,13},{6,14},{7,15},{8,0},{9,1},... | collective-permute-start | bytes 196616 | tf_op jit(solution)/shard_map/ppermute | solution.py:252
  38.0 8.8 %collective-permute-start.11 = (bf16[128,256]{1,0:T(8,128)(2,1)S(1)}, bf16[128,256]{1,0:T(8,128)(2,1)S(1)}, u32[]{:S(2)}, u32[]{:S(2)}) collective-permute-start(bf16[128,256]{1,0:T(8,128)(2,1)S(1)} %get-tuple-element.61), channel_id=1, source_target_pairs={{0,9},{1,8},{2,11},{3,10},{4,13},{5,12},{6,15},{7,14},{8,1},{9,0},... | collective-permute-start | bytes 196616 | tf_op jit(solution)/shard_map/ppermute | solution.py:252
  40.5 8.4 %collective-permute-start.12 = (bf16[128,256]{1,0:T(8,128)(2,1)S(1)}, bf16[128,256]{1,0:T(8,128)(2,1)S(1)}, u32[]{:S(2)}, u32[]{:S(2)}) collective-permute-start(bf16[128,256]{1,0:T(8,128)(2,1)S(1)} %get-tuple-element.62), channel_id=1, source_target_pairs={{0,10},{1,11},{2,8},{3,9},{4,14},{5,15},{6,12},{7,13},{8,2},{9,3},... | collective-permute-start | bytes 196616 | tf_op jit(solution)/shard_map/ppermute | solution.py:252
  46.9 17.6 %collective-permute-start.13 = (bf16[128,256]{1,0:T(8,128)(2,1)S(1)}, bf16[128,256]{1,0:T(8,128)(2,1)S(1)}, u32[]{:S(2)}, u32[]{:S(2)}) collective-permute-start(bf16[128,256]{1,0:T(8,128)(2,1)S(1)} %get-tuple-element.63), channel_id=1, source_target_pairs={{0,11},{1,10},{2,9},{3,8},{4,15},{5,14},{6,13},{7,12},{8,3},{9,2},... | collective-permute-start | bytes 196616 | tf_op jit(solution)/shard_map/ppermute | solution.py:252
  48.9 15.6 %collective-permute-start.14 = (bf16[128,256]{1,0:T(8,128)(2,1)S(1)}, bf16[128,256]{1,0:T(8,128)(2,1)S(1)}, u32[]{:S(2)}, u32[]{:S(2)}) collective-permute-start(bf16[128,256]{1,0:T(8,128)(2,1)S(1)} %get-tuple-element.64), channel_id=1, source_target_pairs={{0,12},{1,13},{2,14},{3,15},{4,8},{5,9},{6,10},{7,11},{8,4},{9,5},... | collective-permute-start | bytes 196616 | tf_op jit(solution)/shard_map/ppermute | solution.py:252
  51.1 13.4 %collective-permute-start.15 = (bf16[128,256]{1,0:T(8,128)(2,1)S(1)}, bf16[128,256]{1,0:T(8,128)(2,1)S(1)}, u32[]{:S(2)}, u32[]{:S(2)}) collective-permute-start(bf16[128,256]{1,0:T(8,128)(2,1)S(1)} %get-tuple-element.65), channel_id=1, source_target_pairs={{0,13},{1,12},{2,15},{3,14},{4,9},{5,8},{6,11},{7,10},{8,5},{9,4},... | collective-permute-start | bytes 196616 | tf_op jit(solution)/shard_map/ppermute | solution.py:252
  56.6 7.9 %collective-permute-start.16 = (bf16[128,256]{1,0:T(8,128)(2,1)S(1)}, bf16[128,256]{1,0:T(8,128)(2,1)S(1)}, u32[]{:S(2)}, u32[]{:S(2)}) collective-permute-start(bf16[128,256]{1,0:T(8,128)(2,1)S(1)} %get-tuple-element.66), channel_id=1, source_target_pairs={{0,14},{1,15},{2,12},{3,13},{4,10},{5,11},{6,8},{7,9},{8,6},{9,7},... | collective-permute-start | bytes 196616 | tf_op jit(solution)/shard_map/ppermute | solution.py:252
  56.6 7.9 %collective-permute-start.17 = (bf16[128,256]{1,0:T(8,128)(2,1)S(1)}, bf16[128,256]{1,0:T(8,128)(2,1)S(1)}, u32[]{:S(2)}, u32[]{:S(2)}) collective-permute-start(bf16[128,256]{1,0:T(8,128)(2,1)S(1)} %get-tuple-element.67), channel_id=1, source_target_pairs={{0,15},{1,14},{2,13},{3,12},{4,11},{5,10},{6,9},{7,8},{8,7},{9,6},... | collective-permute-start | bytes 196616 | tf_op jit(solution)/shard_map/ppermute | solution.py:252
  65.9 6.9 %collective-permute-start.18 = (bf16[128,256]{1,0:T(8,128)(2,1)S(1)}, bf16[128,256]{1,0:T(8,128)(2,1)S(1)}, u32[]{:S(2)}, u32[]{:S(2)}) collective-permute-start(bf16[128,256]{1,0:T(8,128)(2,1)S(1)} %get-tuple-element.69), channel_id=1, source_target_pairs={{0,1},{1,0},{2,3},{3,2},{4,5},{5,4},{6,7},{7,6},{8,9},{9,8},{10,11... | collective-permute-start | bytes 196616 | tf_op jit(solution)/shard_map/ppermute | solution.py:252
  69.6 5.3 %collective-permute-start.19 = (bf16[128,256]{1,0:T(8,128)(2,1)S(1)}, bf16[128,256]{1,0:T(8,128)(2,1)S(1)}, u32[]{:S(2)}, u32[]{:S(2)}) collective-permute-start(bf16[128,256]{1,0:T(8,128)(2,1)S(1)} %get-tuple-element.70), channel_id=1, source_target_pairs={{0,2},{1,3},{2,0},{3,1},{4,6},{5,7},{6,4},{7,5},{8,10},{9,11},{10,... | collective-permute-start | bytes 196616 | tf_op jit(solution)/shard_map/ppermute | solution.py:252
  69.6 5.3 %collective-permute-start.20 = (bf16[128,256]{1,0:T(8,128)(2,1)S(1)}, bf16[128,256]{1,0:T(8,128)(2,1)S(1)}, u32[]{:S(2)}, u32[]{:S(2)}) collective-permute-start(bf16[128,256]{1,0:T(8,128)(2,1)S(1)} %get-tuple-element.71), channel_id=1, source_target_pairs={{0,3},{1,2},{2,1},{3,0},{4,7},{5,6},{6,5},{7,4},{8,11},{9,10},{10,... | collective-permute-start | bytes 196616 | tf_op jit(solution)/shard_map/ppermute | solution.py:252
  72.8 3.1 %collective-permute-start.22 = (bf16[128,256]{1,0:T(8,128)(2,1)S(1)}, bf16[128,256]{1,0:T(8,128)(2,1)S(1)}, u32[]{:S(2)}, u32[]{:S(2)}) collective-permute-start(bf16[128,256]{1,0:T(8,128)(2,1)S(1)} %get-tuple-element.77), channel_id=1, source_target_pairs={{0,2},{1,3},{2,0},{3,1},{4,6},{5,7},{6,4},{7,5},{8,10},{9,11},{10,... | collective-permute-start | bytes 196616 | tf_op jit(solution)/shard_map/ppermute | solution.py:252
  72.9 5.2 %collective-permute-start.23 = (bf16[128,256]{1,0:T(8,128)(2,1)S(1)}, bf16[128,256]{1,0:T(8,128)(2,1)S(1)}, u32[]{:S(2)}, u32[]{:S(2)}) collective-permute-start(bf16[128,256]{1,0:T(8,128)(2,1)S(1)} %get-tuple-element.78), channel_id=1, source_target_pairs={{0,3},{1,2},{2,1},{3,0},{4,7},{5,6},{6,5},{7,4},{8,11},{9,10},{10,... | collective-permute-start | bytes 196616 | tf_op jit(solution)/shard_map/ppermute | solution.py:252
  (5 other events, 34.8 us)
